TPU v7x, 256 devices: a whole 4x4x8 slice. The times are simulated.
256 devices in a mesh: dom: 64 (over z, y, core), grp: 4 (over x).
Axes of the slice: x: 4, y: 4, z: 8, core: 2. Of those that a mesh axis runs over, the one named last changes fastest.
Arguments:
- element_faces: int32 [4, 8192], P(None, 'dom'), may hold values from 0 to 8191, as said below
- interior_load: bfloat16 [80, 8192], P(None, 'dom'), may hold values from -6 to 6
- inverses: bfloat16 [80, 80, 8192], P('grp', None, 'dom'), may hold values from -0.625 to 0.625
- lift_operator: float32 [80, 240], P('grp'), may hold values from -0.625 to 0.625
- face_area: float32 [4, 8192], P(None, 'dom'), may hold values from 0.3 to 27
- columns: int32 [7, 8192], P(None, 'dom'), may hold values from -1 to 8191, as said below
- blocks: float32 [7, 60, 60, 8192], P(None, 'grp', None, 'dom'), may hold values from -0.00119 to 0.00119
- diagonal: float32 [60, 8192], P('grp', 'dom'), may hold values from 1.02 to 1.3
Outputs:
- solution: float32 [60, 8192], P('grp', 'dom')
- residual: float32 [60, 8192], P('grp', 'dom')
Inputs may be any that keep to these rules, and one draw needn't show every extreme that they name: `element_faces`: every face block of an element is owned by the element's own index of dom or the one before or after it; an index owns the face blocks i * 128 to (i + 1) * 128 - 1. `columns`: slot 0 of a face block row holds the block itself. Every other nonnegative entry is a face block owned by the row's own index of dom or the one before or after it, and within one slot no number appears twice.
All inputs are finite; a program needn't handle non-finite values.
Results may differ from a plain program's by a relative error of at most 0.0003.
Values sent between devices are 32-bit elements; how exact they have to be, the bound alone decides.
A program may use at most 64 MiB of HBM per device.

v0:
```python
import jax
import jax.numpy as jnp
from jax import lax
from jax.sharding import Mesh
from jax.sharding import PartitionSpec as P

ITERS = 8
DOM = ("dom_0", "dom_1", "dom_2")
DOM_GRP = ("dom_0", "dom_1", "dom_2", "grp")


def in_order(blocks, dim):
    blocks = jnp.moveaxis(blocks, 0, dim)
    dims = blocks.shape
    return blocks.reshape(*dims[:dim], dims[dim] * dims[dim + 1], *dims[dim + 2 :])


def copy_for_each(value, axis):
    copies = jnp.broadcast_to(value, (lax.axis_size(axis), *value.shape))
    return lax.all_to_all(copies, axis, split_axis=0, concat_axis=0, tiled=True)


def gather_directly(value, axis, dim):
    return in_order(copy_for_each(value, axis), dim)


def padded(cells, sides, width):
    for axis, dim in sides:
        count = lax.axis_size(axis)
        ends = count - 1
        head = lax.slice_in_dim(cells, 0, width, axis=dim)
        tail = lax.slice_in_dim(cells, cells.shape[dim] - width, cells.shape[dim], axis=dim)
        cells = jnp.concatenate(
            [
                lax.ppermute(tail, axis, [(i, (i + 1) % count) for i in range(ends)]),
                cells,
                lax.ppermute(head, axis, [((i + 1) % count, i) for i in range(ends)]),
            ],
            axis=dim,
        )
    return cells


def shifted(block, axis, distance):
    devices = range(lax.axis_size(axis))
    route = [(i - distance, i) for i in devices if i - distance in devices]
    return lax.ppermute(block, axis, route)


def cut_along(value, dim, count):
    before, after = (value.shape[:dim], value.shape[dim + 1 :])
    return jnp.moveaxis(value.reshape(*before, count, -1, *after), dim, 0)


def summed_on_arrival(value, axis, dim):
    count = lax.axis_size(axis)
    blocks = lax.all_to_all(cut_along(value, dim, count), axis, 0, 0, tiled=True)
    return jnp.sum(blocks, axis=0)


def by_axis(value, axes):
    for axis in axes:
        value = lax.psum(value, axis)
    return value


def spread(field_rows):
    faces_here = field_rows.shape[1]
    whole = gather_directly(field_rows, "grp", 0)
    return padded(whole, ((DOM, 1),), faces_here)


def deliver(slab):
    faces_here = slab.shape[1] // 3
    from_upper = shifted(slab[:, :faces_here], DOM, -1)
    from_lower = shifted(slab[:, 2 * faces_here :], DOM, 1)
    summed = slab[:, faces_here : 2 * faces_here] + from_upper + from_lower
    return summed_on_arrival(summed, "grp", 0)


def to_slab(entries, targets, faces_here):
    return jax.ops.segment_sum(entries, targets.reshape(-1), num_segments=3 * faces_here).T


def operate(field_rows, blocks, local_index, usable, diagonal):
    slab = spread(field_rows)
    picked = jnp.where(usable[None, :, :], slab[:, local_index], jnp.zeros((), jnp.float32))
    forward = jnp.einsum("sijf,jsf->if", blocks, picked, precision=lax.Precision.HIGHEST)
    transposed = jnp.einsum("sijf,if->sjf", blocks, field_rows, precision=lax.Precision.HIGHEST)
    transposed = jnp.where(usable[:, None, :], transposed, jnp.zeros((), jnp.float32))
    slot_count, height, faces_here = transposed.shape
    entries = jnp.transpose(transposed, (0, 2, 1)).reshape(slot_count * faces_here, height)
    return diagonal * field_rows + forward + deliver(to_slab(entries, local_index, faces_here))


def two_products(residual, image):
    return (
        by_axis(jnp.sum(residual * residual), DOM_GRP),
        by_axis(jnp.sum(residual * image), DOM_GRP),
    )


def on_device(
    element_faces, interior_load, inverses, lift_operator, face_area, columns, blocks, diagonal
):
    domain = lax.axis_index(DOM)
    faces_here = diagonal.shape[1]
    full_width = lift_operator.shape[1] // 4
    elements_here = interior_load.shape[1]
    u_rows = jnp.einsum("ije,je->ie", inverses, interior_load, preferred_element_type=jnp.float32)
    lifted = lax.dot_general(
        lift_operator, u_rows, (((0,), (0,)), ((), ())), precision=lax.Precision.HIGHEST
    )
    contrib = -(lifted.reshape(4, full_width, elements_here) * face_area[:, None, :])
    entries = jnp.transpose(contrib, (0, 2, 1)).reshape(4 * elements_here, full_width)
    slot_faces = element_faces - (domain - 1) * faces_here
    right_side = deliver(to_slab(entries, slot_faces, faces_here))
    usable = columns >= 0
    local_index = jnp.where(usable, columns - (domain - 1) * faces_here, faces_here)
    solution = jnp.zeros_like(right_side)
    residual = right_side
    image = operate(residual, blocks, local_index, usable, diagonal)
    norm_now, product_sum = two_products(residual, image)
    alpha = norm_now / product_sum
    direction, along = (residual, image)
    for iteration in range(ITERS):
        solution = solution + alpha * direction
        residual = residual - alpha * along
        if iteration + 1 < ITERS:
            image = operate(residual, blocks, local_index, usable, diagonal)
            norm_next, product_sum = two_products(residual, image)
            ratio = norm_next / norm_now
            alpha = norm_next / (product_sum - ratio * norm_next / alpha)
            direction = residual + ratio * direction
            along = image + ratio * along
            norm_now = norm_next
    return (solution, residual)


def solution(mesh):
    torus = Mesh(
        mesh.devices.reshape(8, 4, 2, mesh.shape["grp"]), ("dom_0", "dom_1", "dom_2", "grp")
    )
    placed = (
        P(None, DOM),
        P(None, DOM),
        P("grp", None, DOM),
        P("grp", None),
        P(None, DOM),
        P(None, DOM),
        P(None, "grp", None, DOM),
        P("grp", DOM),
    )
    return jax.shard_map(
        on_device,
        mesh=torus,
        in_specs=placed,
        out_specs=(P("grp", DOM), P("grp", DOM)),
        check_vma=False,
    )
```

profile of v0, /device:TPU:1, one launch (start us, length us, event | category | flops | bytes accessed | tf_op | source)
XLA Modules:
  0.0 879.1 jit_solution(18303853080815893465)
XLA Ops:
  82.0 22.0 %all-reduce.7 = (f32[]{:T(128)}, f32[]{:T(128)}) all-reduce(f32[]{:T(128)} %get-tuple-element.17, f32[]{:T(128)} %get-tuple-element.16), channel_id=1, replica_groups=mesh['dom_0'=8,'dom_1'=4,'dom_2'=2,'grp'=4] {'dom_0'}, use_global_device_ids=true, to_apply=%region_3.4 | all-reduce | flops 2 | bytes 16 | tf_op jit(solution)/shard_map/psum | solution.py:63
  104.0 10.7 %all-reduce.23 = (f32[]{:T(128)}, f32[]{:T(128)}) all-reduce(f32[]{:T(128)} %get-tuple-element.32, f32[]{:T(128)} %get-tuple-element.33), channel_id=1, replica_groups=mesh['dom_0'=8,'dom_1'=4,'dom_2'=2,'grp'=4] {'dom_1'}, use_global_device_ids=true, to_apply=%region_4.5 | all-reduce | flops 2 | bytes 16 | tf_op jit(solution)/shard_map/psum | solution.py:63
  114.7 10.2 %all-reduce.31 = (f32[]{:T(128)}, f32[]{:T(128)}) all-reduce(f32[]{:T(128)} %get-tuple-element.64, f32[]{:T(128)} %get-tuple-element.65), channel_id=1, replica_groups=mesh['dom_0'=8,'dom_1'=4,'dom_2'=2,'grp'=4] {'dom_2'}, use_global_device_ids=true, to_apply=%region_5.6 | all-reduce | flops 2 | bytes 16 | tf_op jit(solution)/shard_map/psum | solution.py:63
  124.9 7.5 all-reduce.15
  190.9 14.1 %all-reduce.6 = (f32[]{:T(128)}, f32[]{:T(128)}) all-reduce(f32[]{:T(128)} %get-tuple-element.15, f32[]{:T(128)} %get-tuple-element.14), channel_id=1, replica_groups=mesh['dom_0'=8,'dom_1'=4,'dom_2'=2,'grp'=4] {'dom_0'}, use_global_device_ids=true, to_apply=%region_15.16 | all-reduce | flops 2 | bytes 16 | tf_op jit(solution)/shard_map/psum | solution.py:63
  205.0 10.3 %all-reduce.22 = (f32[]{:T(128)}, f32[]{:T(128)}) all-reduce(f32[]{:T(128)} %get-tuple-element.30, f32[]{:T(128)} %get-tuple-element.31), channel_id=1, replica_groups=mesh['dom_0'=8,'dom_1'=4,'dom_2'=2,'grp'=4] {'dom_1'}, use_global_device_ids=true, to_apply=%region_16.17 | all-reduce | flops 2 | bytes 16 | tf_op jit(solution)/shard_map/psum | solution.py:63
  215.3 9.5 %all-reduce.30 = (f32[]{:T(128)}, f32[]{:T(128)}) all-reduce(f32[]{:T(128)} %get-tuple-element.62, f32[]{:T(128)} %get-tuple-element.63), channel_id=1, replica_groups=mesh['dom_0'=8,'dom_1'=4,'dom_2'=2,'grp'=4] {'dom_2'}, use_global_device_ids=true, to_apply=%region_17.18 | all-reduce | flops 2 | bytes 16 | tf_op jit(solution)/shard_map/psum | solution.py:63
  224.8 7.5 all-reduce.14
  294.8 14.1 %all-reduce.5 = (f32[]{:T(128)}, f32[]{:T(128)}) all-reduce(f32[]{:T(128)} %get-tuple-element.13, f32[]{:T(128)} %get-tuple-element.12), channel_id=1, replica_groups=mesh['dom_0'=8,'dom_1'=4,'dom_2'=2,'grp'=4] {'dom_0'}, use_global_device_ids=true, to_apply=%region_27.28 | all-reduce | flops 2 | bytes 16 | tf_op jit(solution)/shard_map/psum | solution.py:63
  308.9 10.0 %all-reduce.21 = (f32[]{:T(128)}, f32[]{:T(128)}) all-reduce(f32[]{:T(128)} %get-tuple-element.28, f32[]{:T(128)} %get-tuple-element.29), channel_id=1, replica_groups=mesh['dom_0'=8,'dom_1'=4,'dom_2'=2,'grp'=4] {'dom_1'}, use_global_device_ids=true, to_apply=%region_28.29 | all-reduce | flops 2 | bytes 16 | tf_op jit(solution)/shard_map/psum | solution.py:63
  318.9 10.2 %all-reduce.29 = (f32[]{:T(128)}, f32[]{:T(128)}) all-reduce(f32[]{:T(128)} %get-tuple-element.60, f32[]{:T(128)} %get-tuple-element.61), channel_id=1, replica_groups=mesh['dom_0'=8,'dom_1'=4,'dom_2'=2,'grp'=4] {'dom_2'}, use_global_device_ids=true, to_apply=%region_29.30 | all-reduce | flops 2 | bytes 16 | tf_op jit(solution)/shard_map/psum | solution.py:63
  329.1 7.5 all-reduce.13
  401.9 14.1 %all-reduce.4 = (f32[]{:T(128)}, f32[]{:T(128)}) all-reduce(f32[]{:T(128)} %get-tuple-element.11, f32[]{:T(128)} %get-tuple-element.10), channel_id=1, replica_groups=mesh['dom_0'=8,'dom_1'=4,'dom_2'=2,'grp'=4] {'dom_0'}, use_global_device_ids=true, to_apply=%region_39.40 | all-reduce | flops 2 | bytes 16 | tf_op jit(solution)/shard_map/psum | solution.py:63
  416.0 9.9 %all-reduce.20 = (f32[]{:T(128)}, f32[]{:T(128)}) all-reduce(f32[]{:T(128)} %get-tuple-element.26, f32[]{:T(128)} %get-tuple-element.27), channel_id=1, replica_groups=mesh['dom_0'=8,'dom_1'=4,'dom_2'=2,'grp'=4] {'dom_1'}, use_global_device_ids=true, to_apply=%region_40.41 | all-reduce | flops 2 | bytes 16 | tf_op jit(solution)/shard_map/psum | solution.py:63
  425.9 10.2 %all-reduce.28 = (f32[]{:T(128)}, f32[]{:T(128)}) all-reduce(f32[]{:T(128)} %get-tuple-element.58, f32[]{:T(128)} %get-tuple-element.59), channel_id=1, replica_groups=mesh['dom_0'=8,'dom_1'=4,'dom_2'=2,'grp'=4] {'dom_2'}, use_global_device_ids=true, to_apply=%region_41.42 | all-reduce | flops 2 | bytes 16 | tf_op jit(solution)/shard_map/psum | solution.py:63
  436.1 7.5 all-reduce.12
  508.4 14.1 %all-reduce.3 = (f32[]{:T(128)}, f32[]{:T(128)}) all-reduce(f32[]{:T(128)} %get-tuple-element.9, f32[]{:T(128)} %get-tuple-element.8), channel_id=1, replica_groups=mesh['dom_0'=8,'dom_1'=4,'dom_2'=2,'grp'=4] {'dom_0'}, use_global_device_ids=true, to_apply=%region_51.52 | all-reduce | flops 2 | bytes 16 | tf_op jit(solution)/shard_map/psum | solution.py:63
  522.5 10.0 %all-reduce.19 = (f32[]{:T(128)}, f32[]{:T(128)}) all-reduce(f32[]{:T(128)} %get-tuple-element.24, f32[]{:T(128)} %get-tuple-element.25), channel_id=1, replica_groups=mesh['dom_0'=8,'dom_1'=4,'dom_2'=2,'grp'=4] {'dom_1'}, use_global_device_ids=true, to_apply=%region_52.53 | all-reduce | flops 2 | bytes 16 | tf_op jit(solution)/shard_map/psum | solution.py:63
  532.4 10.2 %all-reduce.27 = (f32[]{:T(128)}, f32[]{:T(128)}) all-reduce(f32[]{:T(128)} %get-tuple-element.56, f32[]{:T(128)} %get-tuple-element.57), channel_id=1, replica_groups=mesh['dom_0'=8,'dom_1'=4,'dom_2'=2,'grp'=4] {'dom_2'}, use_global_device_ids=true, to_apply=%region_53.54 | all-reduce | flops 2 | bytes 16 | tf_op jit(solution)/shard_map/psum | solution.py:63
  542.7 7.5 all-reduce.11
  616.8 14.1 %all-reduce.2 = (f32[]{:T(128)}, f32[]{:T(128)}) all-reduce(f32[]{:T(128)} %get-tuple-element.7, f32[]{:T(128)} %get-tuple-element.6), channel_id=1, replica_groups=mesh['dom_0'=8,'dom_1'=4,'dom_2'=2,'grp'=4] {'dom_0'}, use_global_device_ids=true, to_apply=%region_63.64 | all-reduce | flops 2 | bytes 16 | tf_op jit(solution)/shard_map/psum | solution.py:63
  630.9 9.9 %all-reduce.18 = (f32[]{:T(128)}, f32[]{:T(128)}) all-reduce(f32[]{:T(128)} %get-tuple-element.22, f32[]{:T(128)} %get-tuple-element.23), channel_id=1, replica_groups=mesh['dom_0'=8,'dom_1'=4,'dom_2'=2,'grp'=4] {'dom_1'}, use_global_device_ids=true, to_apply=%region_64.65 | all-reduce | flops 2 | bytes 16 | tf_op jit(solution)/shard_map/psum | solution.py:63
  640.8 10.2 %all-reduce.26 = (f32[]{:T(128)}, f32[]{:T(128)}) all-reduce(f32[]{:T(128)} %get-tuple-element.54, f32[]{:T(128)} %get-tuple-element.55), channel_id=1, replica_groups=mesh['dom_0'=8,'dom_1'=4,'dom_2'=2,'grp'=4] {'dom_2'}, use_global_device_ids=true, to_apply=%region_65.66 | all-reduce | flops 2 | bytes 16 | tf_op jit(solution)/shard_map/psum | solution.py:63
  651.0 7.5 all-reduce.10
  723.1 14.0 %all-reduce.1 = (f32[]{:T(128)}, f32[]{:T(128)}) all-reduce(f32[]{:T(128)} %get-tuple-element.5, f32[]{:T(128)} %get-tuple-element.4), channel_id=1, replica_groups=mesh['dom_0'=8,'dom_1'=4,'dom_2'=2,'grp'=4] {'dom_0'}, use_global_device_ids=true, to_apply=%region_75.76 | all-reduce | flops 2 | bytes 16 | tf_op jit(solution)/shard_map/psum | solution.py:63
  737.2 10.0 %all-reduce.17 = (f32[]{:T(128)}, f32[]{:T(128)}) all-reduce(f32[]{:T(128)} %get-tuple-element.20, f32[]{:T(128)} %get-tuple-element.21), channel_id=1, replica_groups=mesh['dom_0'=8,'dom_1'=4,'dom_2'=2,'grp'=4] {'dom_1'}, use_global_device_ids=true, to_apply=%region_76.77 | all-reduce | flops 2 | bytes 16 | tf_op jit(solution)/shard_map/psum | solution.py:63
  747.2 10.2 %all-reduce.25 = (f32[]{:T(128)}, f32[]{:T(128)}) all-reduce(f32[]{:T(128)} %get-tuple-element.52, f32[]{:T(128)} %get-tuple-element.53), channel_id=1, replica_groups=mesh['dom_0'=8,'dom_1'=4,'dom_2'=2,'grp'=4] {'dom_2'}, use_global_device_ids=true, to_apply=%region_77.78 | all-reduce | flops 2 | bytes 16 | tf_op jit(solution)/shard_map/psum | solution.py:63
  757.3 7.5 all-reduce.9
  831.0 14.0 %all-reduce = (f32[]{:T(128)}, f32[]{:T(128)}) all-reduce(f32[]{:T(128)} %get-tuple-element.3, f32[]{:T(128)} %get-tuple-element.2), channel_id=1, replica_groups=mesh['dom_0'=8,'dom_1'=4,'dom_2'=2,'grp'=4] {'dom_0'}, use_global_device_ids=true, to_apply=%region_87.88 | all-reduce | flops 2 | bytes 16 | tf_op jit(solution)/shard_map/psum | solution.py:63
  845.0 10.0 %all-reduce.16 = (f32[]{:T(128)}, f32[]{:T(128)}) all-reduce(f32[]{:T(128)} %get-tuple-element.18, f32[]{:T(128)} %get-tuple-element.19), channel_id=1, replica_groups=mesh['dom_0'=8,'dom_1'=4,'dom_2'=2,'grp'=4] {'dom_1'}, use_global_device_ids=true, to_apply=%region_88.89 | all-reduce | flops 2 | bytes 16 | tf_op jit(solution)/shard_map/psum | solution.py:63
  855.0 10.2 %all-reduce.24 = (f32[]{:T(128)}, f32[]{:T(128)}) all-reduce(f32[]{:T(128)} %get-tuple-element.50, f32[]{:T(128)} %get-tuple-element.51), channel_id=1, replica_groups=mesh['dom_0'=8,'dom_1'=4,'dom_2'=2,'grp'=4] {'dom_2'}, use_global_device_ids=true, to_apply=%region_89.90 | all-reduce | flops 2 | bytes 16 | tf_op jit(solution)/shard_map/psum | solution.py:63
  865.2 7.6 all-reduce.8
  (298 shorter events, 506.4 us)
Async XLA Ops:
  6.8 7.8 collective-permute-start
  15.9 7.8 all-to-all-start
  24.3 7.5 all-to-all-start.1
  32.5 11.9 %collective-permute-start.3 = (f32[60,128]{0,1:T(8,128)}, f32[60,128]{0,1:T(8,128)S(1)}, u32[]{:S(2)}, u32[]{:S(2)}) collective-permute-start(f32[60,128]{0,1:T(8,128)} %copy.54), channel_id=1, source_target_pairs={{4,0},{8,4},{12,8},{16,12},{20,16},{24,20},{28,24},{32,28},{36,32}... | collective-permute-start | bytes 92168 | tf_op jit(solution)/shard_map/ppermute | solution.py:37
  36.6 7.8 collective-permute-start.2
  63.6 7.2 collective-permute-start.4
  73.8 7.5 all-to-all-start.2
  142.6 10.2 %collective-permute-start.7 = (f32[60,128]{0,1:T(8,128)}, f32[60,128]{0,1:T(8,128)S(1)}, u32[]{:S(2)}, u32[]{:S(2)}) collective-permute-start(f32[60,128]{0,1:T(8,128)} %copy.60), channel_id=1, source_target_pairs={{4,0},{8,4},{12,8},{16,12},{20,16},{24,20},{28,24},{32,28},{36,32}... | collective-permute-start | bytes 92168 | tf_op jit(solution)/shard_map/ppermute | solution.py:37
  171.4 8.2 collective-permute-start.8
  173.4 6.3 collective-permute-start.9
  182.7 7.5 all-to-all-start.4
  245.7 10.2 %collective-permute-start.11 = (f32[60,128]{0,1:T(8,128)}, f32[60,128]{0,1:T(8,128)S(1)}, u32[]{:S(2)}, u32[]{:S(2)}) collective-permute-start(f32[60,128]{0,1:T(8,128)} %copy.66), channel_id=1, source_target_pairs={{4,0},{8,4},{12,8},{16,12},{20,16},{24,20},{28,24},{32,28},{36,32}... | collective-permute-start | bytes 92168 | tf_op jit(solution)/shard_map/ppermute | solution.py:37
  274.5 7.8 collective-permute-start.12
  276.5 5.8 collective-permute-start.13
  285.3 7.5 all-to-all-start.6
  351.3 10.2 %collective-permute-start.15 = (f32[60,128]{0,1:T(8,128)}, f32[60,128]{0,1:T(8,128)S(1)}, u32[]{:S(2)}, u32[]{:S(2)}) collective-permute-start(f32[60,128]{0,1:T(8,128)} %copy.72), channel_id=1, source_target_pairs={{4,0},{8,4},{12,8},{16,12},{20,16},{24,20},{28,24},{32,28},{36,32}... | collective-permute-start | bytes 92168 | tf_op jit(solution)/shard_map/ppermute | solution.py:37
  380.1 7.8 collective-permute-start.16
  382.1 5.8 collective-permute-start.17
  392.3 8.2 all-to-all-start.8
  457.7 10.4 %collective-permute-start.19 = (f32[60,128]{0,1:T(8,128)}, f32[60,128]{0,1:T(8,128)S(1)}, u32[]{:S(2)}, u32[]{:S(2)}) collective-permute-start(f32[60,128]{0,1:T(8,128)} %copy.78), channel_id=1, source_target_pairs={{4,0},{8,4},{12,8},{16,12},{20,16},{24,20},{28,24},{32,28},{36,32}... | collective-permute-start | bytes 92168 | tf_op jit(solution)/shard_map/ppermute | solution.py:37
  486.6 7.8 collective-permute-start.20
  488.6 5.8 collective-permute-start.21
  498.8 8.2 all-to-all-start.10
  564.9 10.2 %collective-permute-start.23 = (f32[60,128]{0,1:T(8,128)}, f32[60,128]{0,1:T(8,128)S(1)}, u32[]{:S(2)}, u32[]{:S(2)}) collective-permute-start(f32[60,128]{0,1:T(8,128)} %copy.84), channel_id=1, source_target_pairs={{4,0},{8,4},{12,8},{16,12},{20,16},{24,20},{28,24},{32,28},{36,32}... | collective-permute-start | bytes 92168 | tf_op jit(solution)/shard_map/ppermute | solution.py:37
  593.7 7.8 collective-permute-start.24
  605.9 8.2 all-to-all-start.12
  672.4 10.4 %collective-permute-start.27 = (f32[60,128]{0,1:T(8,128)}, f32[60,128]{0,1:T(8,128)S(1)}, u32[]{:S(2)}, u32[]{:S(2)}) collective-permute-start(f32[60,128]{0,1:T(8,128)} %copy.90), channel_id=1, source_target_pairs={{4,0},{8,4},{12,8},{16,12},{20,16},{24,20},{28,24},{32,28},{36,32}... | collective-permute-start | bytes 92168 | tf_op jit(solution)/shard_map/ppermute | solution.py:37
  701.3 7.8 collective-permute-start.28
  713.5 8.2 all-to-all-start.14
  779.6 10.2 %collective-permute-start.31 = (f32[60,128]{0,1:T(8,128)}, f32[60,128]{0,1:T(8,128)S(1)}, u32[]{:S(2)}, u32[]{:S(2)}) collective-permute-start(f32[60,128]{0,1:T(8,128)} %copy.96), channel_id=1, source_target_pairs={{4,0},{8,4},{12,8},{16,12},{20,16},{24,20},{28,24},{32,28},{36,32}... | collective-permute-start | bytes 92168 | tf_op jit(solution)/shard_map/ppermute | solution.py:37
  808.4 7.8 collective-permute-start.32
  820.6 8.2 all-to-all-start.16
  (29 other events, 800.0 us)
where the time goes:
time: 897 us; the launch traced here: 879 us
  blocking collectives  394 us (44%)
  starting transfers between devices  164 us (18%)
  other arithmetic  137 us (15%)
  local copies, waits for them, and re-layouts  119 us (13%)
  waiting for transfers between devices  35 us (4%)
  between operations  30.3 us (3%)
    psum x32, blocking collectives, by_axis(): value = lax.psum(value, axis)  342 us
    scatter-add x9, other arithmetic, to_slab(): jax.ops.segment_sum(entries, targets.reshape(-1), num_segments=3 * faces_...  58.8 us
    ppermute x18, starting transfers between devices, shifted(): return lax.ppermute(block, axis, route)  55.7 us
    all_to_all x7, blocking collectives, copy_for_each(): return lax.all_to_all(copies, axis, split_axis=0, concat_axis=0, tiled=True)  51.3 us
    gather x16, local copies, waits for them, and re-layouts, operate(): slab[:, local_index]  44.8 us
    ppermute x8, starting transfers between devices, padded(): lax.ppermute(head, axis, [((i + 1) % count, i) for i in range(ends)])  42.8 us
    all_to_all x9, starting transfers between devices, summed_on_arrival(): lax.all_to_all(cut_along(value, dim, count), axis, 0, 0, tiled=True)  32.6 us
    ppermute x8, starting transfers between devices, padded(): lax.ppermute(tail, axis, [(i, (i + 1) % count) for i in range(ends)])  29.8 us
  transfers between devices with their start and end apart: 44, of which 18 were waited for; matrix products, arithmetic and copies ran while one was open for 4% of the time, Pallas kernels for 0%

commit v1 on v0

v1 whole, which is shorter than its diff:
```python
import jax
import jax.numpy as jnp
from jax import lax
from jax.experimental import pallas as pl
from jax.experimental.pallas import tpu as pltpu
from jax.sharding import PartitionSpec as P

MESH = pl.DeviceIdType.MESH
F32 = jnp.float32
SHIFT = 1.16
FAR_FIRST = (2, 1, 3, 0)
LINKS = [(s, h) for h in FAR_FIRST for s in (1, -1)] + [(0, 2), (0, 1), (0, 3)]


def wide(row, rows):
    return jnp.broadcast_to(row, (rows, row.shape[-1]))


def pick(value, lanes):
    return jnp.take_along_axis(value, lanes, axis=1, mode="promise_in_bounds")


def kernel(
    n_dom, n_grp, faces_all,
    faces_h, load_h, inv_h, lift_h, area_h, cols_h, raw_h, diag_h,
    sol_ref, res_ref,
    faces, load, inv, lift, area, cols, raw, diag,
    blk, dg, lanes_of, part_of, back, slab, vrecv, tsend, trecv, ra, rb, st, cs,
    in_sem, vs_sem, vr_sem, ts_sem, tr_sem, as_sem, ar_sem, bs_sem, br_sem,
):
    d, g = lax.axis_index("dom"), lax.axis_index("grp")
    core = lax.rem(d, 2)
    y = lax.rem(d // 2, 4)
    z = d // 8
    zs = n_dom // 8
    slots = blk.shape[0]

    loads = [
        pltpu.make_async_copy(a, b, in_sem.at[i])
        for i, (a, b) in enumerate(
            [(inv_h, inv), (load_h, load), (lift_h, lift), (area_h, area), (faces_h, faces),
             (cols_h, cols), (diag_h, diag), (raw_h, raw)]
        )
    ]
    for c in loads:
        c.start()

    def link(s, h):
        return lax.rem(d + s + n_dom, n_dom), lax.rem(g + h, n_grp)

    def peer_a(dy, dx):
        y2 = lax.rem(y + dy, 4)
        return (z * 4 + y2) * 2 + core, lax.rem(g + dx, 4)

    def peer_b(dz, dc):
        z2 = lax.rem(z + dz, zs)
        return (z2 * 4 + y) * 2 + lax.rem(core + dc, 2), g

    group_a = [(a, b) for a in range(4) for b in range(4) if (a, b) != (0, 0)]
    group_b = [(a, b) for a in range(zs) for b in range(2) if (a, b) != (0, 0)]

    bar = pltpu.get_barrier_semaphore()
    greeted = (
        [link(s, h) for s, h in LINKS]
        + [peer_a(a, b) for a, b in group_a if a != 0]
        + [peer_b(a, b) for a, b in group_b]
    )
    for who in greeted:
        pl.semaphore_signal(bar, inc=1, device_id=who, device_id_type=MESH)

    def t_copy(par, s, h):
        peer = link(s, h)
        return pltpu.make_async_remote_copy(
            tsend.at[s + 1, peer[1]], trecv.at[par, s + 1, g], ts_sem.at[s + 1, h],
            tr_sem.at[par, s + 1, g], device_id=peer, device_id_type=MESH)

    def t_from(par, s, h):
        src = lax.rem(g + n_grp - h, n_grp)
        return pltpu.make_async_remote_copy(
            tsend.at[s + 1, g], trecv.at[par, s + 1, src], ts_sem.at[s + 1, h],
            tr_sem.at[par, s + 1, src], device_id=link(s, h), device_id_type=MESH)

    def v_copy(par, s, h):
        return pltpu.make_async_remote_copy(
            vrecv.at[par, 1, g], vrecv.at[par, 1 - s, g], vs_sem.at[s + 1, h],
            vr_sem.at[par, 1 - s, g], device_id=link(s, h), device_id_type=MESH)

    def v_from(par, s, h):
        src = lax.rem(g + n_grp - h, n_grp)
        return pltpu.make_async_remote_copy(
            vrecv.at[par, 1, g], vrecv.at[par, 1 - s, src], vs_sem.at[s + 1, h],
            vr_sem.at[par, 1 - s, src], device_id=link(s, h), device_id_type=MESH)

    def deliver_start(par):
        trecv[par, 1, g] = tsend[1, g]
        for s, h in LINKS:
            t_copy(par, s, h).start()

    def deliver_end(par):
        for s, h in LINKS:
            t_from(par, s, h).wait_recv()
        total = trecv[par, 0, 0]
        for s in range(3):
            for k in range(4):
                if (s, k) != (0, 0):
                    total = total + trecv[par, s, k]
        for s, h in LINKS:
            t_copy(par, s, h).wait_send()
        return total

    for c in loads[:5]:
        c.wait()
    interior = jnp.sum(inv[...].astype(F32) * load[...].astype(F32)[None], axis=1)
    base = (d - 1) * 128
    ends = lax.broadcasted_iota(jnp.int32, (384, 128), 0)
    out = jnp.zeros((60, 384), F32)
    for k in range(4):
        lifted = lax.dot_general(
            lift[:, 60 * k : 60 * k + 60], interior, (((0,), (0,)), ((), ())),
            precision=lax.Precision.HIGHEST, preferred_element_type=F32)
        rest = -(lifted * area[k : k + 1])
        hit = (wide(faces[k : k + 1] - base, 384) == ends).astype(F32).astype(jnp.bfloat16)
        for _ in range(3):
            part = rest.astype(jnp.bfloat16)
            rest = rest - part.astype(F32)
            out = out + lax.dot_general(
                part, hit, (((1,), (1,)), ((), ())), preferred_element_type=F32)
    slab[...] = out
    tsend[...] = jnp.zeros(tsend.shape, F32)
    for s in range(3):
        for k in range(4):
            tsend[s, k, 0] = slab[15 * k : 15 * k + 8, 128 * s : 128 * s + 128]
            tsend[s, k, 1, 0:7] = slab[15 * k + 8 : 15 * k + 15, 128 * s : 128 * s + 128]
    pl.semaphore_wait(bar, len(greeted))
    deliver_start(1)

    for c in loads[5:]:
        c.wait()
    dg[...] = jnp.zeros(dg.shape, F32)
    dg[0] = diag[0:8] - SHIFT
    dg[1, 0:7] = diag[8:15] - SHIFT

    blk[...] = jnp.zeros(blk.shape, F32)

    def respace(n, carry):
        s, i = n // 15, lax.rem(n, 15)
        for k in range(4):
            blk[s, i, 2 * k] = raw[s, i, 15 * k : 15 * k + 8]
            blk[s, i, 2 * k + 1, 0:7] = raw[s, i, 15 * k + 8 : 15 * k + 15]
        return carry

    lax.fori_loop(0, slots * 15, respace, 0)
    numbers = lax.broadcasted_iota(jnp.int32, (8, 128), 1).astype(F32) + 1.0
    numbers = numbers.astype(jnp.bfloat16)
    for s in range(1, slots):
        row = cols[s : s + 1]
        there = jnp.where(row >= 0, row - base, -1)
        lanes_of[s - 1] = wide(there & 127, 8)
        part_of[s - 1] = wide(there >> 7, 8)
        hit = (wide(there, 384) == ends).astype(F32).astype(jnp.bfloat16)
        found = lax.dot_general(
            numbers, hit, (((1,), (1,)), ((), ())), preferred_element_type=F32)
        found = found.astype(jnp.int32) - 1
        for k in range(3):
            back[s - 1, k] = found[:, 128 * k : 128 * k + 128]

    def spread8(value):
        return jnp.broadcast_to(value[None], (8, 8, 128)).reshape(64, 128)

    def operate(par, v):
        vrecv[par, 1, g] = v
        for s, h in LINKS:
            v_copy(par, s, h).start()
        rows = v.reshape(16, 128)
        vb = jnp.concatenate([wide(rows[i : i + 1], 8)[None] for i in range(15)], axis=0)
        outs = [None, None, None]
        for s in range(slots):
            turned = jnp.sum(blk[s] * vb[:, None], axis=0).reshape(64, 128)
            if s == 0:
                outs[1] = turned
                continue
            for k in range(3):
                lane = back[s - 1, k]
                moved = pick(turned, spread8(lane & 127))
                moved = jnp.where(spread8(lane) >= 0, moved, 0.0)
                outs[k] = moved if outs[k] is None else outs[k] + moved
        for k in range(3):
            tsend[k] = outs[k].reshape(4, 2, 8, 128)
        deliver_start(par)
        for s, h in LINKS:
            v_from(par, s, h).wait_recv()
        parts = [vrecv[par, k].reshape(64, 128) for k in range(3)]
        acc = jnp.zeros((15, 8, 128), F32)
        for s in range(slots):
            if s == 0:
                taken = parts[1]
            else:
                lane, part = spread8(lanes_of[s - 1]), spread8(part_of[s - 1])
                taken = jnp.zeros((64, 128), F32)
                for k in range(3):
                    taken = jnp.where(part == k, pick(parts[k], lane), taken)
            acc = acc + jnp.sum(blk[s] * taken.reshape(1, 8, 8, 128), axis=1)
        rows = jnp.concatenate([jnp.sum(acc, axis=1), jnp.zeros((1, 128), F32)], axis=0)
        result = dg[...] * v + rows.reshape(2, 8, 128) + deliver_end(par)
        for s, h in LINKS:
            v_copy(par, s, h).wait_send()
        return result

    me_a, me_b = y * 4 + g, z * 2 + core

    def a_copy(par, n):
        return pltpu.make_async_remote_copy(
            ra.at[par, me_a], ra.at[par, me_a], as_sem.at[n], ar_sem.at[par, me_a],
            device_id=peer_a(*group_a[n]), device_id_type=MESH)

    def a_from(par, n):
        dy, dx = group_a[n]
        src = lax.rem(y + 4 - dy, 4) * 4 + lax.rem(g + 4 - dx, 4)
        return pltpu.make_async_remote_copy(
            ra.at[par, me_a], ra.at[par, src], as_sem.at[n], ar_sem.at[par, src],
            device_id=peer_a(dy, dx), device_id_type=MESH)

    def b_copy(par, n):
        return pltpu.make_async_remote_copy(
            rb.at[par, me_b], rb.at[par, me_b], bs_sem.at[n], br_sem.at[par, me_b],
            device_id=peer_b(*group_b[n]), device_id_type=MESH)

    def b_from(par, n):
        dz, dc = group_b[n]
        src = lax.rem(z + zs - dz, zs) * 2 + lax.rem(core + 2 - dc, 2)
        return pltpu.make_async_remote_copy(
            rb.at[par, me_b], rb.at[par, src], bs_sem.at[n], br_sem.at[par, src],
            device_id=peer_b(dz, dc), device_id_type=MESH)

    T0, T1, T2, G0, G1, G2, G3, X, CUR = range(9)

    def sum_start(par):
        basis = [st[T0], st[G0], st[T1], st[G1], st[T2] + st[G2]]
        items = [basis[i] * basis[j] for i in range(5) for j in range(i, 5)] + [dg[...]]
        both = jnp.concatenate([(a[0] + a[1])[None] for a in items], axis=0)
        flat = jnp.sum(jnp.sum(both, axis=1), axis=1, keepdims=True)
        keep = lax.broadcasted_iota(jnp.int32, (16, 128), 0) == lax.broadcasted_iota(
            jnp.int32, (16, 128), 1)
        row = jnp.sum(jnp.where(keep, jnp.broadcast_to(flat, (16, 128)), 0.0), axis=0, keepdims=True)
        ra[par, me_a] = row
        for n in range(len(group_a)):
            a_copy(par, n).start()

    def sum_middle(par):
        for n in range(len(group_a)):
            a_from(par, n).wait_recv()
        rb[par, me_b] = jnp.sum(ra[par], axis=0)
        for n in range(len(group_b)):
            b_copy(par, n).start()
        for n in range(len(group_a)):
            a_copy(par, n).wait_send()

    def sum_end(par):
        for n in range(len(group_b)):
            b_from(par, n).wait_recv()
        total = jnp.sum(rb[par], axis=0)
        for n in range(len(group_b)):
            b_copy(par, n).wait_send()
        return [jnp.broadcast_to(total[:, n : n + 1], (8, 128)) for n in range(16)]

    def two_steps(total):
        shift = cs[...]
        gram = {}
        n = 0
        for i in range(5):
            for j in range(i, 5):
                gram[i, j] = gram[j, i] = total[n]
                n += 1

        def form(a, b):
            whole = None
            for i, left in a.items():
                inner = None
                for j, right in b.items():
                    term = gram[i, j] * right
                    inner = term if inner is None else inner + term
                inner = left * inner
                whole = inner if whole is None else whole + inner
            return whole

        rr0 = gram[0, 0]
        pp = gram[0, 0] + 2.0 * gram[0, 1] + gram[1, 1]
        pbp = gram[0, 2] + gram[0, 3] + gram[1, 2] + gram[1, 3]
        al0 = rr0 / (shift * pp + pbp)
        b, e = -(al0 * shift), -al0
        a = 1.0 + b
        r1 = {0: a, 1: b, 2: e, 3: e}
        rr1 = form(r1, r1)
        be0 = rr1 / rr0
        pa, pb = a + be0, b + be0
        p1 = {0: pa, 1: pb, 2: e, 3: e}
        bp1 = {2: pa, 3: pb, 4: e}
        al1 = rr1 / (shift * form(p1, p1) + form(p1, bp1))
        sc = al1 * shift
        tail = e * (1.0 - sc)
        r2 = {0: a - sc * pa, 1: b - sc * pb, 2: tail - al1 * pa, 3: tail - al1 * pb, 4: -(al1 * e)}
        be1 = form(r2, r2) / rr1
        x0, x1 = al0 + al1 * pa, al0 + al1 * pb
        return r2, (be1 * pa, be1 * pb, be1 * e), (x0, x1, al1 * e)

    r0 = deliver_end(1)
    for n in range(9):
        st[n] = jnp.zeros((2, 8, 128), F32)
    st[T0] = r0
    st[CUR] = r0

    def outer(o, carry):
        par = lax.rem(o, 2)
        sum_start(par)
        first = operate(0, st[CUR])
        sum_middle(par)
        second = operate(1, first + st[G3])
        total = sum_end(par)

        @pl.when(o == 0)
        def _():
            move = total[15] * (1.0 / (60.0 * faces_all))
            cs[...] = move + SHIFT
            inside = lax.broadcasted_iota(jnp.int32, (2, 8, 128), 0) * 8 + lax.broadcasted_iota(
                jnp.int32, (2, 8, 128), 1) < 15
            dg[...] = jnp.where(inside, dg[...] - move[None], 0.0)
            t0 = st[T0]
            t1 = first - move * t0
            t2 = second - move * (first + t1)
            st[T1], st[T2], st[CUR] = t1, t2, t2

        @pl.when(o > 0)
        def _():
            r2, gg, xx = two_steps(total)
            t = [st[T0], st[T1], st[T2], first]
            q = [st[G0], st[G1], st[G2], st[G3]]
            h = [None, t[1] + q[1], t[2] + q[2], t[3] + q[3], second]
            st[X] = st[X] + xx[0] * t[0] + xx[1] * q[0] + xx[2] * h[1]
            for k, n in enumerate((T0, T1, T2)):
                new = (r2[4] * h[k + 2] + r2[2] * t[k + 1] + r2[3] * q[k + 1]
                       + r2[0] * t[k] + r2[1] * q[k])
                st[n] = new
                if n == T2:
                    st[CUR] = new
            for k, n in enumerate((G0, G1, G2, G3)):
                st[n] = gg[2] * h[k + 1] + gg[0] * t[k] + gg[1] * q[k]

        return carry

    lax.fori_loop(0, 4, outer, 0)
    sum_start(0)
    sum_middle(0)
    r2, gg, xx = two_steps(sum_end(0))
    t, q = [st[T0], st[T1], st[T2]], [st[G0], st[G1], st[G2]]
    x = st[X] + xx[0] * t[0] + xx[1] * q[0] + xx[2] * (t[1] + q[1])
    r = (r2[4] * (t[2] + q[2]) + r2[2] * t[1] + r2[3] * q[1] + r2[0] * t[0] + r2[1] * q[0])
    sol_ref[...] = x.reshape(16, 128)[0:15]
    res_ref[...] = r.reshape(16, 128)[0:15]


def solution(mesh):
    n_dom, n_grp = mesh.shape["dom"], mesh.shape["grp"]

    def on_device(element_faces, interior_load, inverses, lift_operator, face_area, columns, blocks, diagonal):
        args = (element_faces, interior_load, inverses, lift_operator, face_area, columns, blocks, diagonal)
        order = (0, 1, 2, 3, 4, 5, 6, 7)
        slots, zs = columns.shape[0], n_dom // 8
        dma, vmem = pltpu.SemaphoreType.DMA, pltpu.VMEM
        faces_all = float(diagonal.shape[1] * n_dom)

        def body(*refs):
            kernel(n_dom, n_grp, faces_all, *refs)

        return pl.pallas_call(
            body,
            out_shape=(jax.ShapeDtypeStruct(diagonal.shape, F32),) * 2,
            in_specs=[pl.BlockSpec(memory_space=pl.ANY)] * 8,
            out_specs=(pl.BlockSpec(memory_space=pltpu.VMEM),) * 2,
            scratch_shapes=[vmem(args[i].shape, args[i].dtype) for i in order]
            + [
                vmem((slots, 15, 8, 8, 128), F32),
                vmem((2, 8, 128), F32),
                vmem((slots - 1, 8, 128), jnp.int32),
                vmem((slots - 1, 8, 128), jnp.int32),
                vmem((slots - 1, 3, 8, 128), jnp.int32),
                vmem((60, 384), F32),
                vmem((2, 3, 4, 2, 8, 128), F32),
                vmem((3, 4, 2, 8, 128), F32),
                vmem((2, 3, 4, 2, 8, 128), F32),
                vmem((2, 16, 1, 128), F32),
                vmem((2, 2 * zs, 1, 128), F32),
                vmem((9, 2, 8, 128), F32),
                vmem((8, 128), F32),
                dma((8,)), dma((3, 4)), dma((2, 3, 4)), dma((3, 4)), dma((2, 3, 4)),
                dma((15,)), dma((2, 16)), dma((2 * zs - 1,)), dma((2, 2 * zs)),
            ],
            compiler_params=pltpu.CompilerParams(
                collective_id=0, has_side_effects=True, vmem_limit_bytes=40 * 1024 * 1024),
            name="cg",
        )(*args)

    return jax.shard_map(
        on_device,
        mesh=mesh,
        in_specs=(
            P(None, "dom"), P(None, "dom"), P("grp", None, "dom"), P("grp", None), P(None, "dom"),
            P(None, "dom"), P(None, "grp", None, "dom"), P("grp", "dom"),
        ),
        out_specs=(P("grp", "dom"), P("grp", "dom")),
        check_vma=False,
    )
```

time: 897 us -> 82.9 us (0.09); the launches traced: 879 us -> 82.5 us
  blocking collectives: 394 us -> 0 us
  starting transfers between devices: 164 us -> 0 us
  other arithmetic: 137 us -> 0 us
  local copies, waits for them, and re-layouts: 119 us -> 8.37 us
  Pallas kernels: 0 us -> 73.5 us
  waiting for transfers between devices: 35 us -> 0 us
  between operations: 30.3 us -> 0.66 us
    psum x32 -> x0, blocking collectives: 342 us -> none  [by_axis(): value = lax.psum(value, axis)]
    ppermute x34 -> x0, starting transfers between devices: 128 us -> none  [the longest x18 55.7 us: shifted(): return lax.ppermute(block, axis, route)]
    pallas_call x0 -> x1, Pallas kernels: none -> 73.5 us  [on_device(): pl.pallas_call(body, out_shape=(jax.ShapeDtypeStruct(diagonal.shape, F32)...]
    scatter-add x9 -> x0, other arithmetic: 58.8 us -> none  [to_slab(): jax.ops.segment_sum(entries, targets.reshape(-1), num_segments=3 * faces_...]
    all_to_all x7 -> x0, blocking collectives: 51.3 us -> none  [copy_for_each(): return lax.all_to_all(copies, axis, split_axis=0, concat_axis=0, tiled=True)]
    gather x16 -> x0, local copies, waits for them, and re-layouts: 44.8 us -> none  [operate(): slab[:, local_index]]
    reshape x35 -> x0, local copies, waits for them, and re-layouts: 42.7 us -> none  [the longest x16 17.9 us: in_order(): blocks.reshape(*dims[:dim], dims[dim] * dims[dim + 1], *dims[dim + 2:])]
    all_to_all x10 -> x0, starting transfers between devices: 35.8 us -> none  [the longest x9 32.6 us: summed_on_arrival(): lax.all_to_all(cut_along(value, dim, count), axis, 0, 0, tiled=True)]
  transfers between devices with their start and end apart: 44 -> 0, of which waited for: 18 -> 0; matrix products, arithmetic and copies ran while one was open for 4% -> 0% of each run, Pallas kernels for 0% -> 0%
where the time goes in v1:
time: 82.9 us; the launch traced here: 82.5 us
  Pallas kernels  73.5 us (89%)
  local copies, waits for them, and re-layouts  8.37 us (10%)
    pallas_call x1, Pallas kernels, on_device(): pl.pallas_call(body, out_shape=(jax.ShapeDtypeStruct(diagonal.shape, F32)...  73.5 us
    unnamed x18, local copies, waits for them, and re-layouts  8.37 us

profile of v1, /device:TPU:1, one launch (start us, length us, event | category | flops | bytes accessed | tf_op | source)
XLA Modules:
  0.0 82.5 jit_solution(12817176009071283518)
XLA Ops:
  0.6 0.0 copy-start
  0.6 2.0 %copy-done = f32[7,15,60,128]{3,2,1,0:T(8,128)S(1)} copy-done((f32[7,15,60,128]{3,2,1,0:T(8,128)S(1)}, f32[7,15,60,128]{3,2,1,0:T(8,128)}, u32[]{:S(2)}) %copy-start) | copy-done | bytes 3225624
  2.6 0.0 copy-start.1
  2.6 1.0 %copy-done.1 = bf16[20,80,128]{2,1,0:T(8,128)(2,1)S(1)} copy-done((bf16[20,80,128]{2,1,0:T(8,128)(2,1)S(1)}, bf16[20,80,128]{2,1,0:T(8,128)(2,1)}, u32[]{:S(2)}) %copy-start.1) | copy-done | bytes 409624
  3.6 0.0 copy-start.2
  3.6 0.7 copy-done.2
  4.3 0.0 copy-start.3
  4.3 0.7 copy-done.3
  5.1 0.0 copy-start.4
  5.1 0.7 copy-done.4
  5.8 0.0 copy-start.5
  5.8 0.7 copy-done.5
  6.5 0.0 copy-start.6
  6.5 0.7 copy-done.6
  7.1 0.0 copy-start.7
  7.1 0.7 copy-done.7
  7.8 73.5 %cg.1 = (f32[15,128]{1,0:T(8,128)S(1)}, f32[15,128]{1,0:T(8,128)S(1)}) custom-call(s32[4,128]{1,0:T(4,128)S(1)} %copy-done.6, bf16[80,128]{1,0:T(8,128)(2,1)S(1)} %copy-done.3, bf16[20,80,128]{2,1,0:T(8,128)(2,1)S(1)} %copy-done.1, f32[20,240]{1,0:T(8,128)S(1)} %copy-done.2, f32[4,128]{1,0:T(4,128)S(1)} %copy-done.7, s32[7,128]{1,0:T(8,128)S(1)} %copy-done.5, ...), custom_call_target="tpu_custom_call" | custom-call | tf_op jit(solution)/shard_map/cg/pallas_call | solution.py:374
  81.3 0.6 copy.12
  81.9 0.6 copy.13
Async XLA Ops:
  0.6 2.0 %copy-start = (f32[7,15,60,128]{3,2,1,0:T(8,128)S(1)}, f32[7,15,60,128]{3,2,1,0:T(8,128)}, u32[]{:S(2)}) copy-start(f32[7,15,60,128]{3,2,1,0:T(8,128)} %refs_6_.1) | copy-start | bytes 9676804
  2.6 1.0 %copy-start.1 = (bf16[20,80,128]{2,1,0:T(8,128)(2,1)S(1)}, bf16[20,80,128]{2,1,0:T(8,128)(2,1)}, u32[]{:S(2)}) copy-start(bf16[20,80,128]{2,1,0:T(8,128)(2,1)} %refs_2_.1) | copy-start | bytes 1228804
  3.6 0.7 copy-start.2
  4.3 0.7 copy-start.3
  5.1 0.7 copy-start.4
  5.8 0.7 copy-start.5
  6.5 0.7 copy-start.6
  7.1 0.7 copy-start.7

commit v2 on v1

--- a/solution.py
+++ b/solution.py
@@ -9,6 +9,7 @@
 F32 = jnp.float32
 SHIFT = 1.16
 FAR_FIRST = (2, 1, 3, 0)
+NEAR_FIRST = (0, 1, 3, 2)
 LINKS = [(s, h) for h in FAR_FIRST for s in (1, -1)] + [(0, 2), (0, 1), (0, 3)]
 
 
@@ -25,7 +26,7 @@
     faces_h, load_h, inv_h, lift_h, area_h, cols_h, raw_h, diag_h,
     sol_ref, res_ref,
     faces, load, inv, lift, area, cols, raw, diag,
-    blk, dg, lanes_of, part_of, back, slab, vrecv, tsend, trecv, ra, rb, st, cs,
+    blk, dg, lanes_of, part_of, back, slab, vrecv, tsend, trecv, ra, rb, st, cs, cf,
     in_sem, vs_sem, vr_sem, ts_sem, tr_sem, as_sem, ar_sem, bs_sem, br_sem,
 ):
     d, g = lax.axis_index("dom"), lax.axis_index("grp")
@@ -48,25 +49,38 @@
     def link(s, h):
         return lax.rem(d + s + n_dom, n_dom), lax.rem(g + h, n_grp)
 
-    def peer_a(dy, dx):
-        y2 = lax.rem(y + dy, 4)
-        return (z * 4 + y2) * 2 + core, lax.rem(g + dx, 4)
-
-    def peer_b(dz, dc):
-        z2 = lax.rem(z + dz, zs)
-        return (z2 * 4 + y) * 2 + lax.rem(core + dc, 2), g
-
-    group_a = [(a, b) for a in range(4) for b in range(4) if (a, b) != (0, 0)]
-    group_b = [(a, b) for a in range(zs) for b in range(2) if (a, b) != (0, 0)]
-
+    def peer_a(dy, dx, c):
+        return (z * 4 + lax.rem(y + dy, 4)) * 2 + c, lax.rem(g + dx, 4)
+
+    def peer_b(dz, c):
+        return (lax.rem(z + dz, zs) * 4 + y) * 2 + c, g
+
+    group_a = [(a, b) for a in range(4) for b in range(4)]
     bar = pltpu.get_barrier_semaphore()
-    greeted = (
-        [link(s, h) for s, h in LINKS]
-        + [peer_a(a, b) for a, b in group_a if a != 0]
-        + [peer_b(a, b) for a, b in group_b]
-    )
-    for who in greeted:
+
+    def greet(who):
         pl.semaphore_signal(bar, inc=1, device_id=who, device_id_type=MESH)
+
+    for s, h in LINKS:
+        greet(link(s, h))
+    for a, b in group_a[1:]:
+        greet(peer_a(a, b, 1))
+    for a in range(1, zs):
+        greet(peer_b(a, 1))
+
+    @pl.when(core == 0)
+    def _():
+        greet(peer_a(0, 0, 1))
+        greet(peer_b(0, 1))
+
+    @pl.when(core == 1)
+    def _():
+        for a, b in group_a:
+            greet(peer_a(a, b, 0))
+        for a in range(zs):
+            greet(peer_b(a, 0))
+
+    greetings = len(LINKS) + 16 + zs + core * (14 + zs)
 
     def t_copy(par, s, h):
         peer = link(s, h)
@@ -131,7 +145,7 @@
         for k in range(4):
             tsend[s, k, 0] = slab[15 * k : 15 * k + 8, 128 * s : 128 * s + 128]
             tsend[s, k, 1, 0:7] = slab[15 * k + 8 : 15 * k + 15, 128 * s : 128 * s + 128]
-    pl.semaphore_wait(bar, len(greeted))
+    pl.semaphore_wait(bar, greetings)
     deliver_start(1)
 
     for c in loads[5:]:
@@ -145,8 +159,8 @@
     def respace(n, carry):
         s, i = n // 15, lax.rem(n, 15)
         for k in range(4):
-            blk[s, i, 2 * k] = raw[s, i, 15 * k : 15 * k + 8]
-            blk[s, i, 2 * k + 1, 0:7] = raw[s, i, 15 * k + 8 : 15 * k + 15]
+            blk[s, k, i, 0] = raw[s, i, 15 * k : 15 * k + 8]
+            blk[s, k, i, 1, 0:7] = raw[s, i, 15 * k + 8 : 15 * k + 15]
         return carry
 
     lax.fori_loop(0, slots * 15, respace, 0)
@@ -164,75 +178,87 @@
         for k in range(3):
             back[s - 1, k] = found[:, 128 * k : 128 * k + 128]
 
-    def spread8(value):
-        return jnp.broadcast_to(value[None], (8, 8, 128)).reshape(64, 128)
-
-    def operate(par, v):
+    def twice(value):
+        return jnp.broadcast_to(value[None], (2, 8, 128)).reshape(16, 128)
+
+    def operate(par, v, during, late):
         vrecv[par, 1, g] = v
         for s, h in LINKS:
             v_copy(par, s, h).start()
         rows = v.reshape(16, 128)
         vb = jnp.concatenate([wide(rows[i : i + 1], 8)[None] for i in range(15)], axis=0)
-        outs = [None, None, None]
-        for s in range(slots):
-            turned = jnp.sum(blk[s] * vb[:, None], axis=0).reshape(64, 128)
-            if s == 0:
-                outs[1] = turned
-                continue
-            for k in range(3):
-                lane = back[s - 1, k]
-                moved = pick(turned, spread8(lane & 127))
-                moved = jnp.where(spread8(lane) >= 0, moved, 0.0)
-                outs[k] = moved if outs[k] is None else outs[k] + moved
-        for k in range(3):
-            tsend[k] = outs[k].reshape(4, 2, 8, 128)
-        deliver_start(par)
-        for s, h in LINKS:
-            v_from(par, s, h).wait_recv()
-        parts = [vrecv[par, k].reshape(64, 128) for k in range(3)]
+        for h in FAR_FIRST:
+            k = lax.rem(g + h, n_grp)
+            outs = [None, None, None]
+            for s in range(slots):
+                turned = jnp.sum(blk[s, k] * vb[:, None], axis=0).reshape(16, 128)
+                if s == 0:
+                    outs[1] = turned
+                    continue
+                for p in range(3):
+                    lane = back[s - 1, p]
+                    moved = pick(turned, twice(lane & 127))
+                    moved = jnp.where(twice(lane) >= 0, moved, 0.0)
+                    outs[p] = moved if outs[p] is None else outs[p] + moved
+            for p in range(3):
+                tsend[p, k] = outs[p].reshape(2, 8, 128)
+            if h == 0:
+                trecv[par, 1, g] = outs[1].reshape(2, 8, 128)
+            for s in (1, -1, 0):
+                if (s, h) != (0, 0):
+                    t_copy(par, s, h).start()
+        during()
         acc = jnp.zeros((15, 8, 128), F32)
-        for s in range(slots):
-            if s == 0:
-                taken = parts[1]
-            else:
-                lane, part = spread8(lanes_of[s - 1]), spread8(part_of[s - 1])
-                taken = jnp.zeros((64, 128), F32)
-                for k in range(3):
-                    taken = jnp.where(part == k, pick(parts[k], lane), taken)
-            acc = acc + jnp.sum(blk[s] * taken.reshape(1, 8, 8, 128), axis=1)
+        for h in NEAR_FIRST:
+            k = lax.rem(g + h, n_grp)
+            for s in (0, 1, -1):
+                if (s, h) != (0, 0):
+                    v_from(par, s, (n_grp - h) % n_grp).wait_recv()
+            parts = [vrecv[par, p, k].reshape(16, 128) for p in range(3)]
+            for s in range(slots):
+                if s == 0:
+                    taken = parts[1]
+                else:
+                    lane, part = twice(lanes_of[s - 1]), twice(part_of[s - 1])
+                    taken = jnp.zeros((16, 128), F32)
+                    for p in range(3):
+                        taken = jnp.where(part == p, pick(parts[p], lane), taken)
+                acc = acc + jnp.sum(blk[s, k] * taken.reshape(1, 2, 8, 128), axis=1)
         rows = jnp.concatenate([jnp.sum(acc, axis=1), jnp.zeros((1, 128), F32)], axis=0)
-        result = dg[...] * v + rows.reshape(2, 8, 128) + deliver_end(par)
+        result = dg[...] * v + rows.reshape(2, 8, 128)
+        late()
+        result = result + deliver_end(par)
         for s, h in LINKS:
             v_copy(par, s, h).wait_send()
         return result
 
-    me_a, me_b = y * 4 + g, z * 2 + core
+    me_a = (y * 4 + g) * 2 + core
 
     def a_copy(par, n):
+        dy, dx = group_a[n]
         return pltpu.make_async_remote_copy(
             ra.at[par, me_a], ra.at[par, me_a], as_sem.at[n], ar_sem.at[par, me_a],
-            device_id=peer_a(*group_a[n]), device_id_type=MESH)
-
-    def a_from(par, n):
+            device_id=peer_a(dy, dx, 1), device_id_type=MESH)
+
+    def a_from(par, n, c):
         dy, dx = group_a[n]
-        src = lax.rem(y + 4 - dy, 4) * 4 + lax.rem(g + 4 - dx, 4)
+        src = (lax.rem(y + 4 - dy, 4) * 4 + lax.rem(g + 4 - dx, 4)) * 2 + c
         return pltpu.make_async_remote_copy(
             ra.at[par, me_a], ra.at[par, src], as_sem.at[n], ar_sem.at[par, src],
-            device_id=peer_a(dy, dx), device_id_type=MESH)
-
-    def b_copy(par, n):
-        return pltpu.make_async_remote_copy(
-            rb.at[par, me_b], rb.at[par, me_b], bs_sem.at[n], br_sem.at[par, me_b],
-            device_id=peer_b(*group_b[n]), device_id_type=MESH)
-
-    def b_from(par, n):
-        dz, dc = group_b[n]
-        src = lax.rem(z + zs - dz, zs) * 2 + lax.rem(core + 2 - dc, 2)
-        return pltpu.make_async_remote_copy(
-            rb.at[par, me_b], rb.at[par, src], bs_sem.at[n], br_sem.at[par, src],
-            device_id=peer_b(dz, dc), device_id_type=MESH)
-
-    T0, T1, T2, G0, G1, G2, G3, X, CUR = range(9)
+            device_id=peer_a(dy, dx, 1), device_id_type=MESH)
+
+    def b_copy(par, dz, c):
+        return pltpu.make_async_remote_copy(
+            rb.at[par, z], rb.at[par, z], bs_sem.at[c, dz], br_sem.at[par, z],
+            device_id=peer_b(dz, c), device_id_type=MESH)
+
+    def b_from(par, dz):
+        src = lax.rem(z + zs - dz, zs)
+        return pltpu.make_async_remote_copy(
+            rb.at[par, z], rb.at[par, src], bs_sem.at[0, dz], br_sem.at[par, src],
+            device_id=peer_b(dz, 1 - core), device_id_type=MESH)
+
+    T0, T1, T2, G0, G1, G2, G3, X, CUR, FIRST, SECOND = range(11)
 
     def sum_start(par):
         basis = [st[T0], st[G0], st[T1], st[G1], st[T2] + st[G2]]
@@ -243,24 +269,50 @@
             jnp.int32, (16, 128), 1)
         row = jnp.sum(jnp.where(keep, jnp.broadcast_to(flat, (16, 128)), 0.0), axis=0, keepdims=True)
         ra[par, me_a] = row
-        for n in range(len(group_a)):
+        for n in range(1, 16):
             a_copy(par, n).start()
 
+        @pl.when(core == 0)
+        def _():
+            a_copy(par, 0).start()
+
     def sum_middle(par):
-        for n in range(len(group_a)):
-            a_from(par, n).wait_recv()
-        rb[par, me_b] = jnp.sum(ra[par], axis=0)
-        for n in range(len(group_b)):
-            b_copy(par, n).start()
-        for n in range(len(group_a)):
+        @pl.when(core == 1)
+        def _():
+            for n in range(16):
+                a_from(par, n, 0).wait_recv()
+                if n:
+                    a_from(par, n, 1).wait_recv()
+            rb[par, z] = jnp.sum(ra[par], axis=0)
+            for n in range(1, zs):
+                b_copy(par, n, 0).start()
+                b_copy(par, n, 1).start()
+            b_copy(par, 0, 0).start()
+
+        for n in range(1, 16):
             a_copy(par, n).wait_send()
 
+        @pl.when(core == 0)
+        def _():
+            a_copy(par, 0).wait_send()
+
     def sum_end(par):
-        for n in range(len(group_b)):
+        for n in range(1, zs):
             b_from(par, n).wait_recv()
+
+        @pl.when(core == 0)
+        def _():
+            b_from(par, 0).wait_recv()
+
         total = jnp.sum(rb[par], axis=0)
-        for n in range(len(group_b)):
-            b_copy(par, n).wait_send()
+
+        @pl.when(core == 1)
+        def _():
+            for n in range(1, zs):
+                b_copy(par, n, 0).wait_send()
+                b_copy(par, n, 1).wait_send()
+            b_copy(par, 0, 0).wait_send()
+
         return [jnp.broadcast_to(total[:, n : n + 1], (8, 128)) for n in range(16)]
 
     def two_steps(total):
@@ -303,51 +355,76 @@
         x0, x1 = al0 + al1 * pa, al0 + al1 * pb
         return r2, (be1 * pa, be1 * pb, be1 * e), (x0, x1, al1 * e)
 
+    def advance():
+        c = [cf[n] for n in range(11)]
+        t = [st[T0], st[T1], st[T2], st[FIRST]]
+        q = [st[G0], st[G1], st[G2], st[G3]]
+        h = [None, t[1] + q[1], t[2] + q[2], t[3] + q[3], st[SECOND]]
+        st[X] = st[X] + c[8] * t[0] + c[9] * q[0] + c[10] * h[1]
+        for k, n in enumerate((T0, T1)):
+            st[n] = (c[4] * h[k + 2] + c[2] * t[k + 1] + c[3] * q[k + 1]
+                     + c[0] * t[k] + c[1] * q[k])
+        st[T2] = st[CUR]
+        for k, n in enumerate((G0, G1, G2, G3)):
+            st[n] = c[7] * h[k + 1] + c[5] * t[k] + c[6] * q[k]
+
     r0 = deliver_end(1)
-    for n in range(9):
+    for n in range(11):
         st[n] = jnp.zeros((2, 8, 128), F32)
+        cf[n] = jnp.zeros((8, 128), F32)
+    cf[0] = jnp.ones((8, 128), F32)
     st[T0] = r0
     st[CUR] = r0
 
     def outer(o, carry):
         par = lax.rem(o, 2)
-        sum_start(par)
-        first = operate(0, st[CUR])
-        sum_middle(par)
-        second = operate(1, first + st[G3])
-        total = sum_end(par)
+
+        def open_sum():
+            advance()
+            sum_start(par)
+
+        def close_sum():
+            total = sum_end(par)
+
+            @pl.when(o == 0)
+            def _():
+                cs[...] = total[15] * (1.0 / (60.0 * faces_all)) + SHIFT
+
+            @pl.when(o > 0)
+            def _():
+                r2, gg, xx = two_steps(total)
+                for n in range(5):
+                    cf[n] = r2[n]
+                for n in range(3):
+                    cf[5 + n] = gg[n]
+                    cf[8 + n] = xx[n]
+
+        first = operate(0, st[CUR], open_sum, lambda: None)
+        st[FIRST] = first
+        second = operate(1, first + st[G3], lambda: sum_middle(par), close_sum)
+        st[SECOND] = second
 
         @pl.when(o == 0)
         def _():
-            move = total[15] * (1.0 / (60.0 * faces_all))
-            cs[...] = move + SHIFT
+            move = cs[...] - SHIFT
             inside = lax.broadcasted_iota(jnp.int32, (2, 8, 128), 0) * 8 + lax.broadcasted_iota(
                 jnp.int32, (2, 8, 128), 1) < 15
             dg[...] = jnp.where(inside, dg[...] - move[None], 0.0)
             t0 = st[T0]
             t1 = first - move * t0
             t2 = second - move * (first + t1)
-            st[T1], st[T2], st[CUR] = t1, t2, t2
+            st[T1], st[CUR] = t1, t2
+            st[T2] = t2
 
         @pl.when(o > 0)
         def _():
-            r2, gg, xx = two_steps(total)
-            t = [st[T0], st[T1], st[T2], first]
-            q = [st[G0], st[G1], st[G2], st[G3]]
-            h = [None, t[1] + q[1], t[2] + q[2], t[3] + q[3], second]
-            st[X] = st[X] + xx[0] * t[0] + xx[1] * q[0] + xx[2] * h[1]
-            for k, n in enumerate((T0, T1, T2)):
-                new = (r2[4] * h[k + 2] + r2[2] * t[k + 1] + r2[3] * q[k + 1]
-                       + r2[0] * t[k] + r2[1] * q[k])
-                st[n] = new
-                if n == T2:
-                    st[CUR] = new
-            for k, n in enumerate((G0, G1, G2, G3)):
-                st[n] = gg[2] * h[k + 1] + gg[0] * t[k] + gg[1] * q[k]
+            st[CUR] = (cf[4] * second + cf[2] * first + cf[3] * st[G3]
+                       + cf[0] * st[T2] + cf[1] * st[G2])
 
         return carry
 
     lax.fori_loop(0, 4, outer, 0)
+    advance()
     sum_start(0)
     sum_middle(0)
     r2, gg, xx = two_steps(sum_end(0))
@@ -371,14 +448,14 @@
         def body(*refs):
             kernel(n_dom, n_grp, faces_all, *refs)
 
-        return pl.pallas_call(
+        found = pl.pallas_call(
             body,
             out_shape=(jax.ShapeDtypeStruct(diagonal.shape, F32),) * 2,
             in_specs=[pl.BlockSpec(memory_space=pl.ANY)] * 8,
             out_specs=(pl.BlockSpec(memory_space=pltpu.VMEM),) * 2,
             scratch_shapes=[vmem(args[i].shape, args[i].dtype) for i in order]
             + [
-                vmem((slots, 15, 8, 8, 128), F32),
+                vmem((slots, n_grp, 15, 2, 8, 128), F32),
                 vmem((2, 8, 128), F32),
                 vmem((slots - 1, 8, 128), jnp.int32),
                 vmem((slots - 1, 8, 128), jnp.int32),
@@ -387,17 +464,34 @@
                 vmem((2, 3, 4, 2, 8, 128), F32),
                 vmem((3, 4, 2, 8, 128), F32),
                 vmem((2, 3, 4, 2, 8, 128), F32),
-                vmem((2, 16, 1, 128), F32),
-                vmem((2, 2 * zs, 1, 128), F32),
-                vmem((9, 2, 8, 128), F32),
+                vmem((2, 32, 1, 128), F32),
+                vmem((2, zs, 1, 128), F32),
+                vmem((11, 2, 8, 128), F32),
                 vmem((8, 128), F32),
+                vmem((11, 8, 128), F32),
                 dma((8,)), dma((3, 4)), dma((2, 3, 4)), dma((3, 4)), dma((2, 3, 4)),
-                dma((15,)), dma((2, 16)), dma((2 * zs - 1,)), dma((2, 2 * zs)),
+                dma((16,)), dma((2, 32)), dma((2, zs)), dma((2, zs)),
             ],
             compiler_params=pltpu.CompilerParams(
-                collective_id=0, has_side_effects=True, vmem_limit_bytes=40 * 1024 * 1024),
+                collective_id=0, has_side_effects=True, vmem_limit_bytes=62 * 1024 * 1024),
             name="cg",
         )(*args)
+
+        def hand_over(x, r, x_out, r_out, sem):
+            moves = [pltpu.make_async_copy(x, x_out, sem.at[0]), pltpu.make_async_copy(r, r_out, sem.at[1])]
+            for m in moves:
+                m.start()
+            for m in moves:
+                m.wait()
+
+        return pl.pallas_call(
+            hand_over,
+            out_shape=(jax.ShapeDtypeStruct(diagonal.shape, F32),) * 2,
+            in_specs=[pl.BlockSpec(memory_space=pl.ANY)] * 2,
+            out_specs=(pl.BlockSpec(memory_space=pl.ANY),) * 2,
+            scratch_shapes=[dma((2,))],
+            name="hand_over",
+        )(*found)
 
     return jax.shard_map(
         on_device,

time: 82.9 us -> 73.2 us (0.88)
  local copies, waits for them, and re-layouts: 8.37 us -> 0 us
  Pallas kernels: 73.5 us -> 72.5 us
    unnamed x18 -> x0, local copies, waits for them, and re-layouts: 8.37 us -> none
    pallas_call x1, Pallas kernels: 73.5 us -> 70.9 us  [on_device(): pl.pallas_call(body, out_shape=(jax.ShapeDtypeStruct(diagonal.shape, F32)...]
    pallas_call x0 -> x1, Pallas kernels: none -> 1.59 us  [on_device(): pl.pallas_call(hand_over, out_shape=(jax.ShapeDtypeStruct(diagonal.shape,...]
where the time goes in v2:
time: 73.2 us; the launch traced here: 73.1 us
  Pallas kernels  72.5 us (99%)
    pallas_call x1, Pallas kernels, on_device(): pl.pallas_call(body, out_shape=(jax.ShapeDtypeStruct(diagonal.shape, F32)...  70.9 us
    pallas_call x1, Pallas kernels, on_device(): pl.pallas_call(hand_over, out_shape=(jax.ShapeDtypeStruct(diagonal.shape,...  1.59 us

profile of v2, /device:TPU:1, one launch (start us, length us, event | category | flops | bytes accessed | tf_op | source)
XLA Modules:
  0.0 73.1 jit_solution(12650781335652581575)
XLA Ops:
  0.6 70.9 %cg.1 = (f32[15,128]{1,0:T(8,128)}, f32[15,128]{1,0:T(8,128)}) custom-call(s32[4,128]{1,0:T(4,128)} %refs_0_.1, bf16[80,128]{1,0:T(8,128)(2,1)} %refs_1_.1, bf16[20,80,128]{2,1,0:T(8,128)(2,1)} %refs_2_.1, f32[20,240]{1,0:T(8,128)} %refs_3_.1, f32[4,128]{1,0:T(4,128)} %refs_4_.1, s32[7,128]{1,0:T(8,128)} %refs_5_.1, f32[7,15,60,128]{3,2,1,0:T(8,128)} %refs_6_.1, ...), custom_call_target="tpu_custom_call" | custom-call | tf_op jit(solution)/shard_map/cg/pallas_call | solution.py:451
  71.5 1.6 %hand_over.1 = (f32[15,128]{1,0:T(8,128)}, f32[15,128]{1,0:T(8,128)}) custom-call(f32[15,128]{1,0:T(8,128)} %get-tuple-element.4.x, f32[15,128]{1,0:T(8,128)} %get-tuple-element.5.r), custom_call_target="tpu_custom_call" | custom-call | tf_op jit(solution)/shard_map/hand_over/pallas_call | solution.py:487

commit v3 on v2

--- a/solution.py
+++ b/solution.py
@@ -9,8 +9,9 @@
 F32 = jnp.float32
 SHIFT = 1.16
 FAR_FIRST = (2, 1, 3, 0)
-NEAR_FIRST = (0, 1, 3, 2)
-LINKS = [(s, h) for h in FAR_FIRST for s in (1, -1)] + [(0, 2), (0, 1), (0, 3)]
+A_ORDER = (10, 9, 11, 6, 14, 5, 7, 13, 15, 8, 2, 4, 12, 1, 3)
+OUT, IN, OWN = 1, -1, 0
+LINKS = [(OUT, h) for h in FAR_FIRST] + [(IN, h) for h in FAR_FIRST] + [(OWN, 2), (OWN, 1), (OWN, 3)]
 
 
 def wide(row, rows):
@@ -26,7 +27,7 @@
     faces_h, load_h, inv_h, lift_h, area_h, cols_h, raw_h, diag_h,
     sol_ref, res_ref,
     faces, load, inv, lift, area, cols, raw, diag,
-    blk, dg, lanes_of, part_of, back, slab, vrecv, tsend, trecv, ra, rb, st, cs, cf,
+    blk, dg, lanes_of, part_of, back, slab, vrecv, tsend, trecv, hold, ra, rb, st, cs, cf,
     in_sem, vs_sem, vr_sem, ts_sem, tr_sem, as_sem, ar_sem, bs_sem, br_sem,
 ):
     d, g = lax.axis_index("dom"), lax.axis_index("grp")
@@ -46,7 +47,10 @@
     for c in loads:
         c.start()
 
+    away = 2 * core - 1
+
     def link(s, h):
+        s = s * away
         return lax.rem(d + s + n_dom, n_dom), lax.rem(g + h, n_grp)
 
     def peer_a(dy, dx, c):
@@ -56,6 +60,11 @@
         return (lax.rem(z + dz, zs) * 4 + y) * 2 + c, g
 
     group_a = [(a, b) for a in range(4) for b in range(4)]
+    b_order = sorted(range(1, zs), key=lambda n: -min(n, zs - n))
+    ends_low, ends_high = (3 - g) // 3, g // 3
+    far = [2 + ends_low, 3 - ends_low - 2 * ends_high]
+    far = far + [6 - far[0] - far[1], 0]
+    near = far[::-1]
     bar = pltpu.get_barrier_semaphore()
 
     def greet(who):
@@ -84,26 +93,31 @@
 
     def t_copy(par, s, h):
         peer = link(s, h)
+        s = s * away
         return pltpu.make_async_remote_copy(
             tsend.at[s + 1, peer[1]], trecv.at[par, s + 1, g], ts_sem.at[s + 1, h],
             tr_sem.at[par, s + 1, g], device_id=peer, device_id_type=MESH)
 
     def t_from(par, s, h):
-        src = lax.rem(g + n_grp - h, n_grp)
+        src, peer = lax.rem(g + n_grp - h, n_grp), link(s, h)
+        s = -s * away
         return pltpu.make_async_remote_copy(
             tsend.at[s + 1, g], trecv.at[par, s + 1, src], ts_sem.at[s + 1, h],
-            tr_sem.at[par, s + 1, src], device_id=link(s, h), device_id_type=MESH)
+            tr_sem.at[par, s + 1, src], device_id=peer, device_id_type=MESH)
 
     def v_copy(par, s, h):
+        peer = link(s, h)
+        s = s * away
         return pltpu.make_async_remote_copy(
             vrecv.at[par, 1, g], vrecv.at[par, 1 - s, g], vs_sem.at[s + 1, h],
-            vr_sem.at[par, 1 - s, g], device_id=link(s, h), device_id_type=MESH)
+            vr_sem.at[par, 1 - s, g], device_id=peer, device_id_type=MESH)
 
     def v_from(par, s, h):
-        src = lax.rem(g + n_grp - h, n_grp)
-        return pltpu.make_async_remote_copy(
-            vrecv.at[par, 1, g], vrecv.at[par, 1 - s, src], vs_sem.at[s + 1, h],
-            vr_sem.at[par, 1 - s, src], device_id=link(s, h), device_id_type=MESH)
+        src, peer = lax.rem(g + n_grp - h, n_grp), link(s, h)
+        s = s * away
+        return pltpu.make_async_remote_copy(
+            vrecv.at[par, 1, g], vrecv.at[par, 1 + s, src], vs_sem.at[s + 1, h],
+            vr_sem.at[par, 1 + s, src], device_id=peer, device_id_type=MESH)
 
     def deliver_start(par):
         trecv[par, 1, g] = tsend[1, g]
@@ -181,39 +195,60 @@
     def twice(value):
         return jnp.broadcast_to(value[None], (2, 8, 128)).reshape(16, 128)
 
-    def operate(par, v, during, late):
+    def scatter(s, turned, p):
+        lane = back[s - 1, p]
+        moved = pick(turned.reshape(16, 128), twice(lane & 127))
+        return jnp.where(twice(lane) >= 0, moved, 0.0).reshape(2, 8, 128)
+
+    def operate(par, v, during, late, early):
         vrecv[par, 1, g] = v
-        for s, h in LINKS:
-            v_copy(par, s, h).start()
+        for h in far[:2]:
+            v_copy(par, OUT, h).start()
         rows = v.reshape(16, 128)
         vb = jnp.concatenate([wide(rows[i : i + 1], 8)[None] for i in range(15)], axis=0)
-        for h in FAR_FIRST:
+        for h in far:
             k = lax.rem(g + h, n_grp)
-            outs = [None, None, None]
+            out = None
             for s in range(slots):
-                turned = jnp.sum(blk[s, k] * vb[:, None], axis=0).reshape(16, 128)
-                if s == 0:
-                    outs[1] = turned
-                    continue
-                for p in range(3):
-                    lane = back[s - 1, p]
-                    moved = pick(turned, twice(lane & 127))
-                    moved = jnp.where(twice(lane) >= 0, moved, 0.0)
-                    outs[p] = moved if outs[p] is None else outs[p] + moved
-            for p in range(3):
-                tsend[p, k] = outs[p].reshape(2, 8, 128)
-            if h == 0:
-                trecv[par, 1, g] = outs[1].reshape(2, 8, 128)
-            for s in (1, -1, 0):
-                if (s, h) != (0, 0):
-                    t_copy(par, s, h).start()
-        during()
+                turned = jnp.sum(blk[s, k] * vb[:, None], axis=0)
+                hold[s, k] = turned
+                if s:
+                    moved = scatter(s, turned, 1 + away)
+                    out = moved if out is None else out + moved
+            tsend[1 + away, k] = out
+            t_copy(par, OUT, h).start()
+            if h is far[1]:
+                v_copy(par, OUT, far[2]).start()
+            if h is far[2]:
+                v_copy(par, OUT, far[3]).start()
+        if early:
+            during()
+        for h in far:
+            k = lax.rem(g + h, n_grp)
+            own, inner = hold[0, k], None
+            for s in range(1, slots):
+                turned = hold[s, k]
+                own = own + scatter(s, turned, 1)
+                moved = scatter(s, turned, 1 - away)
+                inner = moved if inner is None else inner + moved
+            tsend[1, k] = own
+            tsend[1 - away, k] = inner
+            if h is not far[3]:
+                v_copy(par, OWN, h).start()
+                t_copy(par, OWN, h).start()
+            else:
+                trecv[par, 1, g] = own
+            v_copy(par, IN, h).start()
+            t_copy(par, IN, h).start()
+        if not early:
+            during()
         acc = jnp.zeros((15, 8, 128), F32)
-        for h in NEAR_FIRST:
+        for h in near:
             k = lax.rem(g + h, n_grp)
-            for s in (0, 1, -1):
-                if (s, h) != (0, 0):
-                    v_from(par, s, (n_grp - h) % n_grp).wait_recv()
+            back_h = lax.rem(n_grp - h, n_grp)
+            for s in (OWN, IN, OUT):
+                if s != OWN or h is not near[0]:
+                    v_from(par, s, back_h).wait_recv()
             parts = [vrecv[par, p, k].reshape(16, 128) for p in range(3)]
             for s in range(slots):
                 if s == 0:
@@ -227,9 +262,17 @@
         rows = jnp.concatenate([jnp.sum(acc, axis=1), jnp.zeros((1, 128), F32)], axis=0)
         result = dg[...] * v + rows.reshape(2, 8, 128)
         late()
-        result = result + deliver_end(par)
         for s, h in LINKS:
+            t_copy(par, s, h).wait_send()
             v_copy(par, s, h).wait_send()
+        result = result + trecv[par, 1, g]
+        for kinds in ((OWN, IN), (OUT,)):
+            for h in near:
+                k = lax.rem(g + h, n_grp)
+                for s in kinds:
+                    if s != OWN or h is not near[0]:
+                        t_from(par, s, lax.rem(n_grp - h, n_grp)).wait_recv()
+                        result = result + trecv[par, 1 - s * away, k]
         return result
 
     me_a = (y * 4 + g) * 2 + core
@@ -258,7 +301,7 @@
             rb.at[par, z], rb.at[par, src], bs_sem.at[0, dz], br_sem.at[par, src],
             device_id=peer_b(dz, 1 - core), device_id_type=MESH)
 
-    T0, T1, T2, G0, G1, G2, G3, X, CUR, FIRST, SECOND = range(11)
+    T0, T1, T2, G0, G1, G2, G3, X = range(8)
 
     def sum_start(par):
         basis = [st[T0], st[G0], st[T1], st[G1], st[T2] + st[G2]]
@@ -269,7 +312,7 @@
             jnp.int32, (16, 128), 1)
         row = jnp.sum(jnp.where(keep, jnp.broadcast_to(flat, (16, 128)), 0.0), axis=0, keepdims=True)
         ra[par, me_a] = row
-        for n in range(1, 16):
+        for n in A_ORDER:
             a_copy(par, n).start()
 
         @pl.when(core == 0)
@@ -284,7 +327,7 @@
                 if n:
                     a_from(par, n, 1).wait_recv()
             rb[par, z] = jnp.sum(ra[par], axis=0)
-            for n in range(1, zs):
+            for n in b_order:
                 b_copy(par, n, 0).start()
                 b_copy(par, n, 1).start()
             b_copy(par, 0, 0).start()
@@ -355,33 +398,30 @@
         x0, x1 = al0 + al1 * pa, al0 + al1 * pb
         return r2, (be1 * pa, be1 * pb, be1 * e), (x0, x1, al1 * e)
 
-    def advance():
-        c = [cf[n] for n in range(11)]
-        t = [st[T0], st[T1], st[T2], st[FIRST]]
+    def advance(total, first):
+        c, gg, xx = two_steps(total)
+        t = [st[T0], st[T1], st[T2], first]
         q = [st[G0], st[G1], st[G2], st[G3]]
-        h = [None, t[1] + q[1], t[2] + q[2], t[3] + q[3], st[SECOND]]
-        st[X] = st[X] + c[8] * t[0] + c[9] * q[0] + c[10] * h[1]
-        for k, n in enumerate((T0, T1)):
-            st[n] = (c[4] * h[k + 2] + c[2] * t[k + 1] + c[3] * q[k + 1]
-                     + c[0] * t[k] + c[1] * q[k])
-        st[T2] = st[CUR]
+        h = [None, t[1] + q[1], t[2] + q[2], t[3] + q[3]]
+        st[X] = st[X] + xx[0] * t[0] + xx[1] * q[0] + xx[2] * h[1]
+        for k, n in enumerate((T0, T1, T2)):
+            new = c[2] * t[k + 1] + c[3] * q[k + 1] + c[0] * t[k] + c[1] * q[k]
+            st[n] = new if n == T2 else new + c[4] * h[k + 2]
         for k, n in enumerate((G0, G1, G2, G3)):
-            st[n] = c[7] * h[k + 1] + c[5] * t[k] + c[6] * q[k]
+            new = gg[0] * t[k] + gg[1] * q[k]
+            st[n] = new if n == G3 else new + gg[2] * h[k + 1]
+        cf[0] = c[4]
+        cf[1] = gg[2]
 
     r0 = deliver_end(1)
-    for n in range(11):
+    for n in range(8):
         st[n] = jnp.zeros((2, 8, 128), F32)
-        cf[n] = jnp.zeros((8, 128), F32)
-    cf[0] = jnp.ones((8, 128), F32)
     st[T0] = r0
-    st[CUR] = r0
+    st[T2] = r0
 
     def outer(o, carry):
         par = lax.rem(o, 2)
-
-        def open_sum():
-            advance()
-            sum_start(par)
+        first = operate(0, st[T2], lambda: sum_start(par), lambda: None, False)
 
         def close_sum():
             total = sum_end(par)
@@ -392,17 +432,9 @@
 
             @pl.when(o > 0)
             def _():
-                r2, gg, xx = two_steps(total)
-                for n in range(5):
-                    cf[n] = r2[n]
-                for n in range(3):
-                    cf[5 + n] = gg[n]
-                    cf[8 + n] = xx[n]
-
-        first = operate(0, st[CUR], open_sum, lambda: None)
-        st[FIRST] = first
-        second = operate(1, first + st[G3], lambda: sum_middle(par), close_sum)
-        st[SECOND] = second
+                advance(total, first)
+
+        second = operate(1, first + st[G3], lambda: sum_middle(par), close_sum, True)
 
         @pl.when(o == 0)
         def _():
@@ -410,21 +442,18 @@
             inside = lax.broadcasted_iota(jnp.int32, (2, 8, 128), 0) * 8 + lax.broadcasted_iota(
                 jnp.int32, (2, 8, 128), 1) < 15
             dg[...] = jnp.where(inside, dg[...] - move[None], 0.0)
-            t0 = st[T0]
-            t1 = first - move * t0
-            t2 = second - move * (first + t1)
-            st[T1], st[CUR] = t1, t2
-            st[T2] = t2
+            t1 = first - move * st[T0]
+            st[T1] = t1
+            st[T2] = second - move * (first + t1)
 
         @pl.when(o > 0)
         def _():
-            st[CUR] = (cf[4] * second + cf[2] * first + cf[3] * st[G3]
-                       + cf[0] * st[T2] + cf[1] * st[G2])
+            st[T2] = st[T2] + cf[0] * second
+            st[G3] = st[G3] + cf[1] * second
 
         return carry
 
     lax.fori_loop(0, 4, outer, 0)
-    advance()
     sum_start(0)
     sum_middle(0)
     r2, gg, xx = two_steps(sum_end(0))
@@ -464,34 +493,21 @@
                 vmem((2, 3, 4, 2, 8, 128), F32),
                 vmem((3, 4, 2, 8, 128), F32),
                 vmem((2, 3, 4, 2, 8, 128), F32),
+                vmem((slots, n_grp, 2, 8, 128), F32),
                 vmem((2, 32, 1, 128), F32),
                 vmem((2, zs, 1, 128), F32),
-                vmem((11, 2, 8, 128), F32),
+                vmem((8, 2, 8, 128), F32),
                 vmem((8, 128), F32),
-                vmem((11, 8, 128), F32),
+                vmem((2, 8, 128), F32),
                 dma((8,)), dma((3, 4)), dma((2, 3, 4)), dma((3, 4)), dma((2, 3, 4)),
                 dma((16,)), dma((2, 32)), dma((2, zs)), dma((2, zs)),
             ],
             compiler_params=pltpu.CompilerParams(
-                collective_id=0, has_side_effects=True, vmem_limit_bytes=62 * 1024 * 1024),
+                collective_id=0, has_side_effects=True, vmem_limit_bytes=40 * 1024 * 1024),
             name="cg",
-        )(*args)
-
-        def hand_over(x, r, x_out, r_out, sem):
-            moves = [pltpu.make_async_copy(x, x_out, sem.at[0]), pltpu.make_async_copy(r, r_out, sem.at[1])]
-            for m in moves:
-                m.start()
-            for m in moves:
-                m.wait()
-
-        return pl.pallas_call(
-            hand_over,
-            out_shape=(jax.ShapeDtypeStruct(diagonal.shape, F32),) * 2,
-            in_specs=[pl.BlockSpec(memory_space=pl.ANY)] * 2,
-            out_specs=(pl.BlockSpec(memory_space=pl.ANY),) * 2,
-            scratch_shapes=[dma((2,))],
-            name="hand_over",
-        )(*found)
+        )(*[pltpu.with_memory_space_constraint(a, pltpu.HBM) for a in args])
+
+        return found
 
     return jax.shard_map(
         on_device,

time: 73.2 us -> 71.7 us (0.980)
  Pallas kernels: 72.5 us -> 69.8 us
  local copies, waits for them, and re-layouts: 0 us -> 1.2 us
    pallas_call x1 -> x0, Pallas kernels: 1.59 us -> none  [on_device(): pl.pallas_call(hand_over, out_shape=(jax.ShapeDtypeStruct(diagonal.shape,...]
    unnamed x0 -> x2, local copies, waits for them, and re-layouts: none -> 1.2 us
    pallas_call x1, Pallas kernels: 70.9 us -> 69.8 us  [on_device(): pl.pallas_call(body, out_shape=(jax.ShapeDtypeStruct(diagonal.shape, F32)...]
where the time goes in v3:
time: 71.7 us; the launch traced here: 71.6 us
  Pallas kernels  69.8 us (97%)
  local copies, waits for them, and re-layouts  1.2 us (2%)
    pallas_call x1, Pallas kernels, on_device(): pl.pallas_call(body, out_shape=(jax.ShapeDtypeStruct(diagonal.shape, F32)...  69.8 us

profile of v3, /device:TPU:1, one launch (start us, length us, event | category | flops | bytes accessed | tf_op | source)
XLA Modules:
  0.0 71.6 jit_solution(15615108868828784829)
XLA Ops:
  0.6 69.8 %cg.1 = (f32[15,128]{1,0:T(8,128)S(1)}, f32[15,128]{1,0:T(8,128)S(1)}) custom-call(s32[4,128]{1,0:T(4,128)} %refs_0_.1, bf16[80,128]{1,0:T(8,128)(2,1)} %refs_1_.1, bf16[20,80,128]{2,1,0:T(8,128)(2,1)} %refs_2_.1, f32[20,240]{1,0:T(8,128)} %refs_3_.1, f32[4,128]{1,0:T(4,128)} %refs_4_.1, s32[7,128]{1,0:T(8,128)} %refs_5_.1, f32[7,15,60,128]{3,2,1,0:T(8,128)} %refs_6_.1, ...), custom_call_target="tpu_custom_call" | custom-call | tf_op jit(solution)/shard_map/cg/pallas_call | solution.py:480
  70.4 0.6 copy.12
  71.0 0.6 copy.13

commit v4 on v3

--- a/solution.py
+++ b/solution.py
@@ -28,7 +28,7 @@
     sol_ref, res_ref,
     faces, load, inv, lift, area, cols, raw, diag,
     blk, dg, lanes_of, part_of, back, slab, vrecv, tsend, trecv, hold, ra, rb, st, cs, cf,
-    in_sem, vs_sem, vr_sem, ts_sem, tr_sem, as_sem, ar_sem, bs_sem, br_sem,
+    in_sem, vs_sem, vr_sem, ts_sem, tr_sem, as_sem, ar_sem, bs_sem, br_sem, ready,
 ):
     d, g = lax.axis_index("dom"), lax.axis_index("grp")
     core = lax.rem(d, 2)
@@ -44,9 +44,6 @@
              (cols_h, cols), (diag_h, diag), (raw_h, raw)]
         )
     ]
-    for c in loads:
-        c.start()
-
     away = 2 * core - 1
 
     def link(s, h):
@@ -70,26 +67,44 @@
     def greet(who):
         pl.semaphore_signal(bar, inc=1, device_id=who, device_id_type=MESH)
 
-    for s, h in LINKS:
-        greet(link(s, h))
-    for a, b in group_a[1:]:
-        greet(peer_a(a, b, 1))
-    for a in range(1, zs):
-        greet(peer_b(a, 1))
-
-    @pl.when(core == 0)
+    edge = (n_dom - 1 - d) // (n_dom - 1) + d // (n_dom - 1)
+
+    def inside(run):
+        pl.when(edge == 0)(run)
+
+    @pl.when(edge == 1)
     def _():
-        greet(peer_a(0, 0, 1))
-        greet(peer_b(0, 1))
+        vrecv[...] = jnp.zeros(vrecv.shape, F32)
+        trecv[...] = jnp.zeros(trecv.shape, F32)
+
+    @inside
+    def _():
+        for h in far:
+            greet(link(OUT, h))
+
 
     @pl.when(core == 1)
     def _():
-        for a, b in group_a:
-            greet(peer_a(a, b, 0))
-        for a in range(zs):
-            greet(peer_b(a, 0))
-
-    greetings = len(LINKS) + 16 + zs + core * (14 + zs)
+        for n in A_ORDER:
+            if n >= 4:
+                greet(peer_a(*group_a[n], 0))
+                greet(peer_a(*group_a[n], 1))
+
+    for s, h in LINKS[4:]:
+        greet(link(s, h))
+    for c in loads:
+        c.start()
+    for n in range(1, zs):
+
+        @pl.when(z + n < zs)
+        def _():
+            greet(peer_b(n, 1))
+
+            @pl.when(core == 1)
+            def _():
+                greet(peer_b(n, 0))
+
+    greetings = len(LINKS) - 4 * edge + 12 + z * (1 + core)
 
     def t_copy(par, s, h):
         peer = link(s, h)
@@ -121,18 +136,30 @@
 
     def deliver_start(par):
         trecv[par, 1, g] = tsend[1, g]
-        for s, h in LINKS:
+
+        @inside
+        def _():
+            for h in far:
+                t_copy(par, OUT, h).start()
+
+        for s, h in LINKS[4:]:
             t_copy(par, s, h).start()
 
     def deliver_end(par):
-        for s, h in LINKS:
+        @inside
+        def _():
+            for s, h in LINKS[:4]:
+                t_from(par, s, h).wait_recv()
+                t_copy(par, s, h).wait_send()
+
+        for s, h in LINKS[4:]:
             t_from(par, s, h).wait_recv()
         total = trecv[par, 0, 0]
         for s in range(3):
             for k in range(4):
                 if (s, k) != (0, 0):
                     total = total + trecv[par, s, k]
-        for s, h in LINKS:
+        for s, h in LINKS[4:]:
             t_copy(par, s, h).wait_send()
         return total
 
@@ -161,6 +188,13 @@
             tsend[s, k, 1, 0:7] = slab[15 * k + 8 : 15 * k + 15, 128 * s : 128 * s + 128]
     pl.semaphore_wait(bar, greetings)
     deliver_start(1)
+    for n in range(1, zs):
+
+        @pl.when(z - n >= 0)
+        def _():
+            who = (((z - n) * 4 + y) * 2 + 1, g)
+            pl.semaphore_signal(ready, inc=1, device_id=who, device_id_type=MESH)
+
 
     for c in loads[5:]:
         c.wait()
@@ -202,8 +236,12 @@
 
     def operate(par, v, during, late, early):
         vrecv[par, 1, g] = v
-        for h in far[:2]:
-            v_copy(par, OUT, h).start()
+
+        @inside
+        def _():
+            for h in far[:2]:
+                v_copy(par, OUT, h).start()
+
         rows = v.reshape(16, 128)
         vb = jnp.concatenate([wide(rows[i : i + 1], 8)[None] for i in range(15)], axis=0)
         for h in far:
@@ -216,11 +254,15 @@
                     moved = scatter(s, turned, 1 + away)
                     out = moved if out is None else out + moved
             tsend[1 + away, k] = out
-            t_copy(par, OUT, h).start()
-            if h is far[1]:
-                v_copy(par, OUT, far[2]).start()
-            if h is far[2]:
-                v_copy(par, OUT, far[3]).start()
+
+            @inside
+            def _():
+                t_copy(par, OUT, h).start()
+                if h is far[1]:
+                    v_copy(par, OUT, far[2]).start()
+                if h is far[2]:
+                    v_copy(par, OUT, far[3]).start()
+
         if early:
             during()
         for h in far:
@@ -246,9 +288,14 @@
         for h in near:
             k = lax.rem(g + h, n_grp)
             back_h = lax.rem(n_grp - h, n_grp)
-            for s in (OWN, IN, OUT):
+            for s in (OWN, IN):
                 if s != OWN or h is not near[0]:
                     v_from(par, s, back_h).wait_recv()
+
+            @inside
+            def _():
+                v_from(par, OUT, back_h).wait_recv()
+
             parts = [vrecv[par, p, k].reshape(16, 128) for p in range(3)]
             for s in range(slots):
                 if s == 0:
@@ -262,17 +309,31 @@
         rows = jnp.concatenate([jnp.sum(acc, axis=1), jnp.zeros((1, 128), F32)], axis=0)
         result = dg[...] * v + rows.reshape(2, 8, 128)
         late()
-        for s, h in LINKS:
+        for s, h in LINKS[4:]:
             t_copy(par, s, h).wait_send()
             v_copy(par, s, h).wait_send()
+
+        @inside
+        def _():
+            for s, h in LINKS[:4]:
+                t_copy(par, s, h).wait_send()
+                v_copy(par, s, h).wait_send()
+
         result = result + trecv[par, 1, g]
-        for kinds in ((OWN, IN), (OUT,)):
+        for h in near:
+            k = lax.rem(g + h, n_grp)
+            for s in (OWN, IN):
+                if s != OWN or h is not near[0]:
+                    t_from(par, s, lax.rem(n_grp - h, n_grp)).wait_recv()
+                    result = result + trecv[par, 1 - s * away, k]
+
+        @inside
+        def _():
             for h in near:
-                k = lax.rem(g + h, n_grp)
-                for s in kinds:
-                    if s != OWN or h is not near[0]:
-                        t_from(par, s, lax.rem(n_grp - h, n_grp)).wait_recv()
-                        result = result + trecv[par, 1 - s * away, k]
+                t_from(par, OUT, lax.rem(n_grp - h, n_grp)).wait_recv()
+
+        for h in near:
+            result = result + trecv[par, 1 - away, lax.rem(g + h, n_grp)]
         return result
 
     me_a = (y * 4 + g) * 2 + core
@@ -421,6 +482,14 @@
 
     def outer(o, carry):
         par = lax.rem(o, 2)
+
+        def middle():
+            @pl.when((o == 0) & (core == 1) & (z < zs - 1))
+            def _():
+                pl.semaphore_wait(ready, 2 * (zs - 1 - z))
+
+            sum_middle(par)
+
         first = operate(0, st[T2], lambda: sum_start(par), lambda: None, False)
 
         def close_sum():
@@ -434,7 +503,7 @@
             def _():
                 advance(total, first)
 
-        second = operate(1, first + st[G3], lambda: sum_middle(par), close_sum, True)
+        second = operate(1, first + st[G3], middle, close_sum, True)
 
         @pl.when(o == 0)
         def _():
@@ -469,7 +538,6 @@
 
     def on_device(element_faces, interior_load, inverses, lift_operator, face_area, columns, blocks, diagonal):
         args = (element_faces, interior_load, inverses, lift_operator, face_area, columns, blocks, diagonal)
-        order = (0, 1, 2, 3, 4, 5, 6, 7)
         slots, zs = columns.shape[0], n_dom // 8
         dma, vmem = pltpu.SemaphoreType.DMA, pltpu.VMEM
         faces_all = float(diagonal.shape[1] * n_dom)
@@ -482,7 +550,7 @@
             out_shape=(jax.ShapeDtypeStruct(diagonal.shape, F32),) * 2,
             in_specs=[pl.BlockSpec(memory_space=pl.ANY)] * 8,
             out_specs=(pl.BlockSpec(memory_space=pltpu.VMEM),) * 2,
-            scratch_shapes=[vmem(args[i].shape, args[i].dtype) for i in order]
+            scratch_shapes=[vmem(a.shape, a.dtype) for a in args]
             + [
                 vmem((slots, n_grp, 15, 2, 8, 128), F32),
                 vmem((2, 8, 128), F32),
@@ -501,6 +569,7 @@
                 vmem((2, 8, 128), F32),
                 dma((8,)), dma((3, 4)), dma((2, 3, 4)), dma((3, 4)), dma((2, 3, 4)),
                 dma((16,)), dma((2, 32)), dma((2, zs)), dma((2, zs)),
+                pltpu.SemaphoreType.REGULAR,
             ],
             compiler_params=pltpu.CompilerParams(
                 collective_id=0, has_side_effects=True, vmem_limit_bytes=40 * 1024 * 1024),

time: 71.7 us -> 71.1 us (level)
  no operation moved by 1% of the time
where the time goes in v4:
time: 71.1 us; the launch traced here: 71 us
  Pallas kernels  69.1 us (97%)
  local copies, waits for them, and re-layouts  1.2 us (2%)
    pallas_call x1, Pallas kernels, on_device(): pl.pallas_call(body, out_shape=(jax.ShapeDtypeStruct(diagonal.shape, F32)...  69.1 us

profile of v4, /device:TPU:1, one launch (start us, length us, event | category | flops | bytes accessed | tf_op | source)
XLA Modules:
  0.0 71.0 jit_solution(5805368766521922345)
XLA Ops:
  0.6 69.1 %cg.1 = (f32[15,128]{1,0:T(8,128)S(1)}, f32[15,128]{1,0:T(8,128)S(1)}) custom-call(s32[4,128]{1,0:T(4,128)} %refs_0_.1, bf16[80,128]{1,0:T(8,128)(2,1)} %refs_1_.1, bf16[20,80,128]{2,1,0:T(8,128)(2,1)} %refs_2_.1, f32[20,240]{1,0:T(8,128)} %refs_3_.1, f32[4,128]{1,0:T(4,128)} %refs_4_.1, s32[7,128]{1,0:T(8,128)} %refs_5_.1, f32[7,15,60,128]{3,2,1,0:T(8,128)} %refs_6_.1, ...), custom_call_target="tpu_custom_call" | custom-call | tf_op jit(solution)/shard_map/cg/pallas_call | solution.py:548
  69.8 0.6 copy.12
  70.4 0.6 copy.13

commit v5 on v4

--- a/solution.py
+++ b/solution.py
@@ -186,32 +186,12 @@
         for k in range(4):
             tsend[s, k, 0] = slab[15 * k : 15 * k + 8, 128 * s : 128 * s + 128]
             tsend[s, k, 1, 0:7] = slab[15 * k + 8 : 15 * k + 15, 128 * s : 128 * s + 128]
-    pl.semaphore_wait(bar, greetings)
-    deliver_start(1)
-    for n in range(1, zs):
-
-        @pl.when(z - n >= 0)
-        def _():
-            who = (((z - n) * 4 + y) * 2 + 1, g)
-            pl.semaphore_signal(ready, inc=1, device_id=who, device_id_type=MESH)
-
-
-    for c in loads[5:]:
+    for c in loads[5:7]:
         c.wait()
     dg[...] = jnp.zeros(dg.shape, F32)
     dg[0] = diag[0:8] - SHIFT
     dg[1, 0:7] = diag[8:15] - SHIFT
 
-    blk[...] = jnp.zeros(blk.shape, F32)
-
-    def respace(n, carry):
-        s, i = n // 15, lax.rem(n, 15)
-        for k in range(4):
-            blk[s, k, i, 0] = raw[s, i, 15 * k : 15 * k + 8]
-            blk[s, k, i, 1, 0:7] = raw[s, i, 15 * k + 8 : 15 * k + 15]
-        return carry
-
-    lax.fori_loop(0, slots * 15, respace, 0)
     numbers = lax.broadcasted_iota(jnp.int32, (8, 128), 1).astype(F32) + 1.0
     numbers = numbers.astype(jnp.bfloat16)
     for s in range(1, slots):
@@ -226,6 +206,29 @@
         for k in range(3):
             back[s - 1, k] = found[:, 128 * k : 128 * k + 128]
 
+    for n in range(8):
+        st[n] = jnp.zeros((2, 8, 128), F32)
+    pl.semaphore_wait(bar, greetings)
+    deliver_start(1)
+    for n in range(1, zs):
+
+        @pl.when(z - n >= 0)
+        def _():
+            who = (((z - n) * 4 + y) * 2 + 1, g)
+            pl.semaphore_signal(ready, inc=1, device_id=who, device_id_type=MESH)
+
+
+    loads[7].wait()
+    blk[...] = jnp.zeros(blk.shape, F32)
+
+    def respace(n, carry):
+        s, i = n // 15, lax.rem(n, 15)
+        for k in range(4):
+            blk[s, k, i, 0] = raw[s, i, 15 * k : 15 * k + 8]
+            blk[s, k, i, 1, 0:7] = raw[s, i, 15 * k + 8 : 15 * k + 15]
+        return carry
+
+    lax.fori_loop(0, slots * 15, respace, 0)
     def twice(value):
         return jnp.broadcast_to(value[None], (2, 8, 128)).reshape(16, 128)
 
@@ -475,8 +478,6 @@
         cf[1] = gg[2]
 
     r0 = deliver_end(1)
-    for n in range(8):
-        st[n] = jnp.zeros((2, 8, 128), F32)
     st[T0] = r0
     st[T2] = r0
 

time: 71.1 us -> 71.2 us (level)
  no operation moved by 1% of the time
where the time goes in v5:
time: 71.2 us; the launch traced here: 71.1 us
  Pallas kernels  69.2 us (97%)
  local copies, waits for them, and re-layouts  1.2 us (2%)
    pallas_call x1, Pallas kernels, on_device(): pl.pallas_call(body, out_shape=(jax.ShapeDtypeStruct(diagonal.shape, F32)...  69.2 us

profile of v5, /device:TPU:1, one launch (start us, length us, event | category | flops | bytes accessed | tf_op | source)
XLA Modules:
  0.0 71.1 jit_solution(2433866813798333945)
XLA Ops:
  0.6 69.2 %cg.1 = (f32[15,128]{1,0:T(8,128)S(1)}, f32[15,128]{1,0:T(8,128)S(1)}) custom-call(s32[4,128]{1,0:T(4,128)} %refs_0_.1, bf16[80,128]{1,0:T(8,128)(2,1)} %refs_1_.1, bf16[20,80,128]{2,1,0:T(8,128)(2,1)} %refs_2_.1, f32[20,240]{1,0:T(8,128)} %refs_3_.1, f32[4,128]{1,0:T(4,128)} %refs_4_.1, s32[7,128]{1,0:T(8,128)} %refs_5_.1, f32[7,15,60,128]{3,2,1,0:T(8,128)} %refs_6_.1, ...), custom_call_target="tpu_custom_call" | custom-call | tf_op jit(solution)/shard_map/cg/pallas_call | solution.py:549
  69.9 0.6 copy.12
  70.5 0.6 copy.13
